TPU v7x, 32 devices: a whole 2x2x4 slice. The times are simulated.
32 devices in a mesh: section: 4 (over y, x), peer: 8 (over z, core).
Axes of the slice: x: 2, y: 2, z: 4, core: 2. Of those that a mesh axis runs over, the one named last changes fastest.
Arguments:
- inbox: bfloat16 [4, 8, 128, 5120], P('section', 'peer'), may hold values from -6 to 6
- routes: int32 [4, 8, 8], replicated, may hold values from 0 to 4, as said below
- adapter_in: bfloat16 [4, 2, 16, 5120], P('section'), may hold values from -0.078125 to 0.078125
- adapter_out: bfloat16 [4, 2, 16, 5120], P('section'), may hold values from -1.5 to 1.5
- returned: bfloat16 [4, 8, 160, 5120], P('section', 'peer'), may hold values from -6 to 6
Outputs:
- handed: bfloat16 [4, 8, 160, 5120], P('section', 'peer')
- mean_in: float32 [4, 2, 16, 5120], P('section', None, None, 'peer')
- mean_out: float32 [4, 2, 16, 5120], P('section', None, None, 'peer')
Inputs may be any that keep to these rules, and one draw needn't show every extreme that they name: routes[s, p, q] is how many micro-batches peer p of section s sends to peer q of the next section; every row sums to 16; every column sums to at most 20, and in every section some column reaches 20; some entry of every section reaches 4.
All inputs are finite; a program needn't handle non-finite values.
Results may differ from a plain program's by a relative error of at most 0.015.
Values may be sent and summed in bfloat16 or wider, within the bound.
No kernel may reach another device: no remote copies, remote signals or barrier semaphores. Data moves between devices by JAX's collectives and lax.ppermute only.
A program may use at most 64 MiB of HBM per device.

v0:
```python
import jax
import jax.numpy as jnp
from jax import lax
from jax.sharding import PartitionSpec as P

D = 5120
MB = 8


epsilon = 1e-06


def from_behind(array, axis, by):
    count = lax.axis_size(axis)
    return lax.ppermute(array, axis, [(i, (i + by) % count) for i in range(count)])


def inverse_rms(hidden):
    return lax.rsqrt(jnp.mean(hidden * hidden, axis=-1, keepdims=True) + epsilon)


def contract_last(left, right):
    return lax.dot_general(
        left, right, (((1,), (1,)), ((), ())), preferred_element_type=jnp.float32
    )


def contract_first(left, right):
    return lax.dot_general(
        left, right, (((0,), (0,)), ((), ())), preferred_element_type=jnp.float32
    )


def section_forward(inputs, weight_in, weight_out):
    hidden = inputs.astype(jnp.float32)
    saved = []
    for layer in range(weight_in.shape[0]):
        scale = inverse_rms(hidden)
        plain = hidden * scale
        normed = plain.astype(jnp.bfloat16)
        lowered = contract_last(normed, weight_in[layer]).astype(jnp.bfloat16)
        saved.append((scale, plain, normed, lowered))
        hidden = hidden + jnp.dot(lowered, weight_out[layer], preferred_element_type=jnp.float32)
    return (hidden.astype(jnp.bfloat16), saved)


def section_backward(saved, weight_in, weight_out, incoming):
    grad = incoming.astype(jnp.float32)
    grads_in = []
    grads_out = []
    for layer in reversed(range(weight_in.shape[0])):
        scale, plain, normed, lowered = saved[layer]
        grad_bf = grad.astype(jnp.bfloat16)
        grads_out.append(contract_first(lowered, grad_bf))
        back_low = contract_last(grad_bf, weight_out[layer]).astype(jnp.bfloat16)
        grads_in.append(contract_first(back_low, normed))
        if layer > 0:
            spread = jnp.dot(back_low, weight_in[layer], preferred_element_type=jnp.float32)
            grad = grad + scale * (
                spread - plain * jnp.mean(spread * plain, axis=-1, keepdims=True)
            )
    return (jnp.stack(grads_in[::-1]), jnp.stack(grads_out[::-1]))


def sender_picks(row, peers, pair, micro):
    sent_end = jnp.cumsum(row)
    sent_start = sent_end - row
    index = jnp.arange(micro, dtype=jnp.int32)
    target = jnp.sum((sent_end[None, :] <= index[:, None]).astype(jnp.int32), axis=1)
    choose = target[:, None] == jnp.arange(peers, dtype=jnp.int32)[None, :]
    offset = index - jnp.sum(jnp.where(choose, sent_start[None, :], 0), axis=1)
    within = offset[:, None] == jnp.arange(pair, dtype=jnp.int32)[None, :]
    picks = choose[:, :, None] & within[:, None, :]
    return picks.reshape(micro, peers * pair).astype(jnp.bfloat16)


def receiver_places(column, peers, pair, capacity):
    slot_start = jnp.cumsum(column) - column
    position = jnp.arange(capacity, dtype=jnp.int32)
    within = jnp.arange(pair, dtype=jnp.int32)
    places = (position[:, None, None] == slot_start[None, :, None] + within[None, None, :]) & (
        within[None, None, :] < column[None, :, None]
    )
    return places.reshape(capacity, peers * pair).astype(jnp.bfloat16)


def route_forward(blocks, table, peer, peers, pair, capacity):
    micro = blocks.shape[0]
    row = lax.dynamic_index_in_dim(table, peer, 0, keepdims=False)
    column = lax.dynamic_index_in_dim(table, peer, 1, keepdims=False)
    picks = sender_picks(row, peers, pair, micro)
    outbound = jnp.einsum("jc,jrd->crd", picks, blocks, preferred_element_type=jnp.float32).astype(
        jnp.bfloat16
    )
    outbound = outbound.reshape(peers, pair * MB, D)
    arrived = lax.all_to_all(outbound, "peer", split_axis=0, concat_axis=0, tiled=True).reshape(
        peers * pair, MB, D
    )
    places = receiver_places(column, peers, pair, capacity)
    return jnp.einsum("kc,crd->krd", places, arrived, preferred_element_type=jnp.float32).astype(
        jnp.bfloat16
    )


def route_backward(slots, table, peer, peers, pair, micro):
    capacity = slots.shape[0]
    row = lax.dynamic_index_in_dim(table, peer, 0, keepdims=False)
    column = lax.dynamic_index_in_dim(table, peer, 1, keepdims=False)
    places = receiver_places(column, peers, pair, capacity)
    spread_out = jnp.einsum(
        "kc,krd->crd", places, slots, preferred_element_type=jnp.float32
    ).astype(jnp.bfloat16)
    spread_out = spread_out.reshape(peers, pair * MB, D)
    arrived = lax.all_to_all(spread_out, "peer", split_axis=0, concat_axis=0, tiled=True).reshape(
        peers * pair, MB, D
    )
    picks = sender_picks(row, peers, pair, micro)
    return jnp.einsum("jc,crd->jrd", picks, arrived, preferred_element_type=jnp.float32).astype(
        jnp.bfloat16
    )


def shards(inbox, routes, adapter_in, adapter_out, returned):
    peers = lax.axis_size("peer")
    section_count = lax.axis_size("section")
    section = lax.axis_index("section")
    peer = lax.axis_index("peer")
    tokens = inbox.shape[2]
    micro = tokens // MB
    pair = max(1, 2 * micro // peers)
    capacity = returned.shape[2] // MB
    weight_in = adapter_in[0]
    weight_out = adapter_out[0]
    earlier = lax.dynamic_index_in_dim(
        routes, (section + section_count - 1) % section_count, 0, keepdims=False
    )
    produced, saved = section_forward(inbox[0, 0], weight_in, weight_out)
    produced = produced.reshape(micro, MB, D)
    slots_here = returned[0, 0].reshape(capacity, MB, D)
    arrived_blocks = from_behind(produced, "section", 1)
    handed = route_forward(arrived_blocks, earlier, peer, peers, pair, capacity)
    gathered_back = route_backward(slots_here, earlier, peer, peers, pair, micro)
    incoming = from_behind(gathered_back, "section", -1)
    terms_in, terms_out = section_backward(
        saved, weight_in, weight_out, incoming.reshape(tokens, D)
    )
    summed_in, summed_out = (
        lax.psum_scatter(
            terms_in.astype(jnp.bfloat16), "peer", scatter_dimension=2, tiled=True
        ).astype(jnp.float32),
        lax.psum_scatter(
            terms_out.astype(jnp.bfloat16), "peer", scatter_dimension=2, tiled=True
        ).astype(jnp.float32),
    )
    mean_in = summed_in / peers
    mean_out = summed_out / peers
    return (handed.reshape(1, 1, capacity * MB, D), mean_in[None], mean_out[None])


def solution(mesh):
    return jax.shard_map(
        shards,
        mesh=mesh,
        in_specs=(
            P("section", "peer", None, None),
            P(),
            P("section", None, None, None),
            P("section", None, None, None),
            P("section", "peer", None, None),
        ),
        out_specs=(
            P("section", "peer", None, None),
            P("section", None, None, "peer"),
            P("section", None, None, "peer"),
        ),
        check_vma=False,
    )
```

profile of v0, /device:TPU:0, one launch (start us, length us, event | category | flops | bytes accessed | tf_op | source)
XLA Modules:
  0.0 217.7 jit_solution(45913586308425294)
XLA Ops:
  7.2 0.9 constant_dynamic-slice_fusion.1
  8.1 0.9 fusion.57
  9.1 0.1 add.92
  9.4 2.9 %convolution_convert_fusion = bf16[32,8,5120]{2,0,1:T(8,128)(2,1)S(1)} fusion(bf16[20,8,5120]{2,1,0:T(8,128)(2,1)S(1)} %bitcast.104, s32[32]{0:T(128)S(1)} %add.95, pred[32]{0:T(512)(128)(4,1)S(1)} %lt.48), kind=kOutput, calls=%fused_computation | convolution fusion | flops 53740800 | bytes 4260000 | tf_op jit(solution)/shard_map/kc,krd->crd/dot_general | solution.py:110
  12.3 2.9 %copy.37 = bf16[32,8,5120]{2,1,0:T(8,128)(2,1)} copy(bf16[32,8,5120]{2,0,1:T(8,128)(2,1)S(1)} %convolution_convert_fusion) | data formatting | bytes 5242880 | tf_op jit(solution)/shard_map/convert_element_type | solution.py:112
  15.2 6.5 %all-to-all-start.1 = ((bf16[8,32,5120]{2,1,0:T(8,128)(2,1)}), bf16[8,32,5120]{2,1,0:T(8,128)(2,1)}, u32[]{:S(2)}, u32[]{:S(2)}) async-start(bf16[8,32,5120]{2,1,0:T(8,128)(2,1)} %bitcast.106), calls=%async_computation.1 | async-start | bytes 5242880 | tf_op jit(solution)/shard_map/all_to_all | solution.py:114
  21.7 0.3 fusion.8
  22.1 1.5 fusion.26
  23.6 0.6 multiply_reduce_fusion.1
  24.3 0.5 convolution_convert_fusion.9
  24.8 0.5 fusion.1
  25.3 0.5 copy-done.1
  25.8 1.8 copy.31
  27.6 1.5 collective-permute-start
  29.1 0.7 fusion.56
  29.8 0.2 reduce-window.8
  29.9 0.1 convert_reduce_fusion
  30.0 0.7 bitcast_subtract_fusion
  30.7 0.1 select_reduce_fusion
  30.9 51.2 %all-to-all-done.1 = bf16[8,32,5120]{2,1,0:T(8,128)(2,1)} async-done(((bf16[8,32,5120]{2,1,0:T(8,128)(2,1)}), bf16[8,32,5120]{2,1,0:T(8,128)(2,1)}, u32[]{:S(2)}, u32[]{:S(2)}) %all-to-all-start.1) | async-done | bytes 2621472 | tf_op jit(solution)/shard_map/all_to_all | solution.py:114
  82.1 5.7 %convolution_convert_fusion.3 = bf16[16,8,5120]{2,0,1:T(8,128)(2,1)} fusion(pred[16,32,1]{0,1,2:T(8,128)(4,1)S(1)} %bitcast.112, bf16[32,8,5120]{2,1,0:T(8,128)(2,1)} %bitcast.19), kind=kOutput, calls=%fused_computation.6 | convolution fusion | flops 42598400 | bytes 3932672 | tf_op jit(solution)/shard_map/jc,crd->jrd/dot_general | solution.py:118
  87.8 2.4 %collective-permute-start.1 = (bf16[16,8,5120]{2,0,1:T(8,128)(2,1)}, bf16[16,8,5120]{2,0,1:T(8,128)(2,1)}, u32[]{:S(2)}, u32[]{:S(2)}) collective-permute-start(bf16[16,8,5120]{2,0,1:T(8,128)(2,1)} %convolution_convert_fusion.3), channel_id=1, source_target_pairs={{0,24},{8,0},{16,8},{24,16},{1,25},{9,1},{17,9},{25,17},{2,26},{10... | collective-permute-start | bytes 3932168 | tf_op jit(solution)/shard_map/ppermute | solution.py:15
  90.3 2.1 convolution_convert_fusion.1
  92.4 3.0 %copy.33 = bf16[32,8,5120]{2,1,0:T(8,128)(2,1)} copy(bf16[32,8,5120]{2,0,1:T(8,128)(2,1)S(1)} %convolution_convert_fusion.1) | data formatting | bytes 5242880 | tf_op jit(solution)/shard_map/convert_element_type | solution.py:92
  95.4 4.4 %all-to-all-start = ((bf16[8,32,5120]{2,1,0:T(8,128)(2,1)}), bf16[8,32,5120]{2,1,0:T(8,128)(2,1)}, u32[]{:S(2)}, u32[]{:S(2)}) async-start(bf16[8,32,5120]{2,1,0:T(8,128)(2,1)} %bitcast.105), calls=%async_computation | async-start | bytes 5242880 | tf_op jit(solution)/shard_map/all_to_all | solution.py:96
  99.8 18.5 %collective-permute-done.1 = bf16[16,8,5120]{2,0,1:T(8,128)(2,1)} collective-permute-done((bf16[16,8,5120]{2,0,1:T(8,128)(2,1)}, bf16[16,8,5120]{2,0,1:T(8,128)(2,1)}, u32[]{:S(2)}, u32[]{:S(2)}) %collective-permute-start.1) | collective-permute-done | bytes 1310752 | tf_op jit(solution)/shard_map/ppermute | solution.py:15
  118.4 2.1 fusion.23
  120.5 2.1 fusion.3
  122.6 0.6 multiply_reduce_fusion
  123.2 3.5 %add_convert_fusion = bf16[128,5120]{1,0:T(8,128)(2,1)} fusion(f32[128,5120]{1,0:T(8,128)S(1)} %get-tuple-element.8, f32[128,5120]{1,0:T(8,128)S(1)} %copy-done.2, f32[128]{0:T(128)S(1)} %broadcast_multiply_fusion, f32[128]{0:T(128)S(1)} %add_rsqrt_fusion, bf16[16,8,5120]{2,0,1:T(8,128)(2,1)} %collective-permute-done.1), kind=kLoop, calls=%fused_computation.25 | loop fusion | flops 4587520 | bytes 7865344 | tf_op jit(solution)/shard_map/convert_element_type | solution.py:53
  126.7 3.0 %fusion.2 = bf16[1,16,5120]{2,1,0:T(8,128)(2,1)} fusion(bf16[1,1,128,5120]{3,2,1,0:T(8,128)(2,1)S(1)} %copy-done.3, f32[128]{0:T(128)S(1)} %add_rsqrt_fusion.1, bf16[128,5120]{1,0:T(8,128)(2,1)} %add_convert_fusion, bf16[1,2,16,5120]{3,2,1,0:T(8,128)(2,1)S(1)} %copy-done.5), kind=kOutput, calls=%fused_computation.12 | convolution fusion | flops 43993088 | bytes 2949632 | tf_op jit(solution)/shard_map/dot_general | solution.py:29
  129.8 0.9 pad_maximum_fusion
  130.7 4.1 %copy.45 = bf16[2,16,5120]{1,0,2:T(2,128)(2,1)} copy(bf16[2,16,5120]{2,1,0:T(8,128)(2,1)S(1)} %pad_maximum_fusion) | data formatting | bytes 655360
  134.8 5.5 %reshape.230 = bf16[5120,32]{1,0:T(8,128)(2,1)} reshape(bf16[5120,2,16]{2,1,0:T(2,128)(2,1)} %bitcast.107) | data formatting | bytes 655360
  140.3 0.3 reduce-scatter.9.cloned.1.call-start
  140.6 0.3 fusion.4
  140.9 2.1 fusion.5
  143.0 4.1 %copy.47 = bf16[2,16,5120]{1,0,2:T(2,128)(2,1)} copy(bf16[2,16,5120]{2,1,0:T(8,128)(2,1)S(1)} %pad_maximum_fusion.1) | data formatting | bytes 655360
  147.1 5.4 %reshape.232 = bf16[5120,32]{1,0:T(8,128)(2,1)} reshape(bf16[5120,2,16]{2,1,0:T(2,128)(2,1)} %bitcast.108) | data formatting | bytes 655360
  152.5 17.6 %all-to-all-done = bf16[8,32,5120]{2,1,0:T(8,128)(2,1)} async-done(((bf16[8,32,5120]{2,1,0:T(8,128)(2,1)}), bf16[8,32,5120]{2,1,0:T(8,128)(2,1)}, u32[]{:S(2)}, u32[]{:S(2)}) %all-to-all-start) | async-done | bytes 2621472 | tf_op jit(solution)/shard_map/all_to_all | solution.py:96
  170.1 4.7 %convolution_convert_fusion.2 = bf16[20,8,5120]{2,0,1:T(8,128)(2,1)S(1)} fusion(bf16[32,8,5120]{2,1,0:T(8,128)(2,1)} %bitcast.14, s32[32]{0:T(128)S(1)} %add.95, pred[32]{0:T(512)(128)(4,1)S(1)} %lt.48), kind=kOutput, calls=%fused_computation.2 | convolution fusion | flops 53249280 | bytes 4260000 | tf_op jit(solution)/shard_map/kc,crd->krd/dot_general | solution.py:100
  174.8 2.1 copy.65
  176.9 1.1 reshape.231
  178.0 0.2 copy.46
  178.1 30.8 %reduce-scatter.9.cloned.1.call-done = bf16[640,32]{1,0:T(8,128)(2,1)} async-done(((bf16[5120,32]{1,0:T(8,128)(2,1)}), bf16[640,32]{1,0:T(8,128)(2,1)}) %reduce-scatter.9.cloned.1.call-update) | async-done | bytes 40976
  208.9 1.1 reshape.233
  210.0 0.2 copy.48
  210.1 0.7 multiply_bitcast_fusion
  (36 shorter events, 0.6 us)
Async XLA Ops:
  7.2 2.3 %copy-start = (bf16[1,1,160,5120]{3,2,1,0:T(8,128)(2,1)S(1)}, bf16[1,1,160,5120]{3,2,1,0:T(8,128)(2,1)}, u32[]{:S(2)}) copy-start(bf16[1,1,160,5120]{3,2,1,0:T(8,128)(2,1)} %param.9) | copy-start | bytes 4915204
  15.2 6.5 %copy-start.3 = (bf16[1,1,128,5120]{3,2,1,0:T(8,128)(2,1)S(1)}, bf16[1,1,128,5120]{3,2,1,0:T(8,128)(2,1)}, u32[]{:S(2)}) copy-start(bf16[1,1,128,5120]{3,2,1,0:T(8,128)(2,1)} %param.5) | copy-start | bytes 3932164
  15.2 66.9 %all-to-all-start.1 = ((bf16[8,32,5120]{2,1,0:T(8,128)(2,1)}), bf16[8,32,5120]{2,1,0:T(8,128)(2,1)}, u32[]{:S(2)}, u32[]{:S(2)}) async-start(bf16[8,32,5120]{2,1,0:T(8,128)(2,1)} %bitcast.106), calls=%async_computation.1 | async-start | bytes 5242880 | tf_op jit(solution)/shard_map/all_to_all | solution.py:114
  21.7 1.9 copy-start.5
  22.1 2.2 copy-start.6
  24.2 1.6 copy-start.1
  27.6 62.7 %collective-permute-start = (bf16[16,8,5120]{2,0,1:T(8,128)(2,1)}, bf16[16,8,5120]{2,0,1:T(8,128)(2,1)}, u32[]{:S(2)}, u32[]{:S(2)}) collective-permute-start(bf16[16,8,5120]{2,0,1:T(8,128)(2,1)} %copy.31), channel_id=1, source_target_pairs={{0,8},{8,16},{16,24},{24,0},{1,9},{9,17},{17,25},{25,1},{2,10},{10... | collective-permute-start | bytes 3932168 | tf_op jit(solution)/shard_map/ppermute | solution.py:15
  87.8 30.5 %collective-permute-start.1 = (bf16[16,8,5120]{2,0,1:T(8,128)(2,1)}, bf16[16,8,5120]{2,0,1:T(8,128)(2,1)}, u32[]{:S(2)}, u32[]{:S(2)}) collective-permute-start(bf16[16,8,5120]{2,0,1:T(8,128)(2,1)} %convolution_convert_fusion.3), channel_id=1, source_target_pairs={{0,24},{8,0},{16,8},{24,16},{1,25},{9,1},{17,9},{25,17},{2,26},{10... | collective-permute-start | bytes 3932168 | tf_op jit(solution)/shard_map/ppermute | solution.py:15
  95.4 74.8 %all-to-all-start = ((bf16[8,32,5120]{2,1,0:T(8,128)(2,1)}), bf16[8,32,5120]{2,1,0:T(8,128)(2,1)}, u32[]{:S(2)}, u32[]{:S(2)}) async-start(bf16[8,32,5120]{2,1,0:T(8,128)(2,1)} %bitcast.105), calls=%async_computation | async-start | bytes 5242880 | tf_op jit(solution)/shard_map/all_to_all | solution.py:96
  99.8 77.1 %reduce-scatter.7.cloned.1.call-start = ((), (), s32[]{:S(2)}) async-start(), calls=%async_computation.4 | async-start | bytes 1474560
  99.8 22.8 %copy-start.2 = (f32[128,5120]{1,0:T(8,128)S(1)}, f32[128,5120]{1,0:T(8,128)}, u32[]{:S(2)}) copy-start(f32[128,5120]{1,0:T(8,128)} %copy-done.1) | copy-start | bytes 7864324
  99.8 22.8 %copy-start.7 = (bf16[1,2,16,5120]{3,2,1,0:T(8,128)(2,1)S(1)}, bf16[1,2,16,5120]{3,2,1,0:T(8,128)(2,1)}, u32[]{:S(2)}) copy-start(bf16[1,2,16,5120]{3,2,1,0:T(8,128)(2,1)} %param.7) | copy-start | bytes 983044
  134.8 5.8 %copy-start.4 = (bf16[128,5120]{1,0:T(8,128)(2,1)S(1)}, bf16[128,5120]{1,0:T(8,128)(2,1)}, u32[]{:S(2)}) copy-start(bf16[128,5120]{1,0:T(8,128)(2,1)} %add_convert_fusion) | copy-start | bytes 3932164
  140.3 68.6 %reduce-scatter.9.cloned.1.call-start = ((), (), s32[]{:S(2)}) async-start(), calls=%async_computation.5 | async-start | bytes 1474560
Sparse Core Ops, SparseCore 0:
  140.4 33.7 reduce-scatter.6
  176.5 32.3 reduce-scatter.8
where the time goes:
time: 219 us; the launch traced here: 218 us
  waiting for transfers between devices  118 us (54%)
  local copies, waits for them, and re-layouts  33.7 us (15%)
  matrix products  28.9 us (13%)
  starting transfers between devices  15.1 us (7%)
  between operations  14.2 us (6%)
  other arithmetic  7.55 us (3%)
    all_to_all x1, waiting for transfers between devices, route_backward(): lax.all_to_all(spread_out, 'peer', split_axis=0, concat_axis=0, tiled=True)  51.2 us
    unnamed x4, waiting for transfers between devices  30.8 us
    unnamed x24, local copies, waits for them, and re-layouts  22 us
    ppermute x2, waiting for transfers between devices, from_behind(): lax.ppermute(array, axis, [(i, (i + by) % count) for i in range(count)])  18.5 us
    all_to_all x1, waiting for transfers between devices, route_forward(): lax.all_to_all(outbound, 'peer', split_axis=0, concat_axis=0, tiled=True)  17.6 us
    dot_general x4, matrix products, contract_first(): lax.dot_general(left, right, (((0,), (0,)), ((), ())), preferred_element_...  7.54 us
    all_to_all x1, starting transfers between devices, route_backward(): lax.all_to_all(spread_out, 'peer', split_axis=0, concat_axis=0, tiled=True)  6.49 us
    dot_general x1, matrix products, route_backward(): jnp.einsum('jc,crd->jrd', picks, arrived, preferred_element_type=jnp.floa...  5.71 us
  transfers between devices with their start and end apart: 6, of which 4 were waited for; matrix products, arithmetic and copies ran while one was open for 27% of the time, Pallas kernels for 0%

commit v1 on v0

v1 whole, which is shorter than its diff:
```python
import functools

import jax
import jax.numpy as jnp
from jax import lax
from jax.experimental import pallas as pl
from jax.experimental.pallas import tpu as pltpu
from jax.sharding import PartitionSpec as P


MB = 8
EPSILON = 1e-06
VMEM_LIMIT = 20 * 2**20
SEND_LIMIT = 8 * 2**20
PREPARE_LIMIT = 12 * 2**20


BF16 = jnp.bfloat16
HBM = pl.BlockSpec(memory_space=pl.ANY)
SMEM = pl.BlockSpec(memory_space=pltpu.SMEM)


class Plan:
    def __init__(self, sections, peers, micro, capacity):
        self.sections, self.peers, self.micro, self.capacity = sections, peers, micro, capacity
        self.chips = peers // 2
        mean = max(1, 2 * micro // peers)
        self.full = 2 * mean
        self.sent = min(self.full, mean + (mean + 1) // 2)
        self.sets = [(0, mean), (mean, self.sent)]
        self.extra = (self.sent, self.full)
        self.spill = min(self.full - self.sent, self.sent - mean)


def hop_pairs(plan, by, offset):
    return [
        (s * plan.peers + p, ((s + by) % plan.sections) * plan.peers + (p ^ offset))
        for s in range(plan.sections)
        for p in range(plan.peers)
    ]


def to_sibling(plan, array):
    return lax.ppermute(array, "peer", [(p, p ^ 1) for p in range(plan.peers)])


def send_kernel(plan, span, weighted, spilling, taking, routes, inbox, *refs):
    chips = plan.chips
    first, end = span
    if weighted:
        weights, refs = refs[:2], refs[2:]
    if taking:
        spilled, refs = refs[0], refs[1:]
    outs, refs = (refs[:chips], refs[chips:]) if end > first else ((), refs)
    if weighted:
        w_out, refs = refs[0], refs[1:]
    if spilling:
        s_out, refs = refs[0], refs[1:]
    stage, sem, out_sem, start, count = refs[:5]
    refs = refs[5:]
    if weighted:
        w_stage, w_sem, refs = refs[0], refs[1], refs[2:]
    if spilling:
        s_stage, s_sem = refs
    section = lax.axis_index("section")
    peer = lax.axis_index("peer")
    chip = lax.div(peer, 2)
    total = jnp.int32(0)
    for c in range(chips):
        load_c = routes[section, peer, 2 * c] + routes[section, peer, 2 * c + 1]
        start[c] = total
        count[c] = load_c
        total = total + load_c

    def pick(e, u):
        return inbox.at[jnp.minimum(start[chip ^ e] + u, plan.micro - 1)]

    def load(e, u):
        return pltpu.make_async_copy(pick(e, u), stage.at[e, u - first], sem.at[e, u - first])

    def store(e):
        return pltpu.make_async_copy(stage.at[e], outs[e], out_sem.at[e])

    if weighted:
        even = lax.rem(peer, 2) == 0
        slots = w_stage.shape[0]
        part = pl.ds(lax.rem(chip, 2) * slots, slots)
        w_load = [pltpu.make_async_copy(weight.at[part], w_stage, w_sem.at[0]) for weight in weights]
        w_store = pltpu.make_async_copy(w_stage, w_out, w_sem.at[1])
        pl.when(even)(lambda: w_load[0].start())
        pl.when(jnp.logical_not(even))(lambda: w_load[1].start())
    order = list(reversed(range(len(outs))))
    for e in order:
        for u in range(first, end):
            if taking and plan.sent - 1 - u < plan.spill:
                own = u < count[chip ^ e]
                other = pltpu.make_async_copy(
                    spilled.at[e, plan.sent - 1 - u], stage.at[e, u - first], sem.at[e, u - first]
                )
                pl.when(own)(lambda: load(e, u).start())
                pl.when(jnp.logical_not(own))(lambda: other.start())
            else:
                load(e, u).start()
    if spilling:
        s_load = [
            pltpu.make_async_copy(pick(e, plan.sent + i), s_stage.at[e, i], s_sem.at[e, i])
            for e in range(chips)
            for i in range(plan.spill)
        ]
        s_store = pltpu.make_async_copy(s_stage, s_out, s_sem.at[chips, 0])
        for copy in s_load:
            copy.start()
    if weighted:
        w_load[0].wait()
        w_store.start()
    for e in order:
        for u in range(first, end):
            load(e, u).wait()
        store(e).start()
    if spilling:
        for copy in s_load:
            copy.wait()
        s_store.start()
    if weighted:
        w_store.wait()
    for e in order:
        store(e).wait()
    if spilling:
        s_store.wait()


def run_send(plan, span, routes, blocks, weights=(), spilling=False, spilled=None):
    width = blocks.shape[-1]
    slots = span[1] - span[0]
    chips = plan.chips if slots else 0
    out_shape = [jax.ShapeDtypeStruct((slots, MB, width), BF16)] * chips
    scratch = [
        pltpu.VMEM((plan.chips, max(1, slots), MB, width), BF16),
        pltpu.SemaphoreType.DMA((plan.chips, max(1, slots))),
        pltpu.SemaphoreType.DMA((plan.chips,)),
        pltpu.SMEM((plan.chips,), jnp.int32),
        pltpu.SMEM((plan.chips,), jnp.int32),
    ]
    if weights:
        quarter = (weights[0].shape[0] // 2, MB, width)
        out_shape.append(jax.ShapeDtypeStruct(quarter, BF16))
        scratch += [pltpu.VMEM(quarter, BF16), pltpu.SemaphoreType.DMA((2,))]
    if spilling:
        spill = (plan.chips, plan.spill, MB, width)
        out_shape.append(jax.ShapeDtypeStruct(spill, BF16))
        scratch += [pltpu.VMEM(spill, BF16), pltpu.SemaphoreType.DMA((plan.chips + 1, plan.spill))]
    taken = () if spilled is None else (spilled,)
    operands = [blocks, *weights, *taken]
    return pl.pallas_call(
        functools.partial(send_kernel, plan, span, bool(weights), spilling, bool(taken)),
        out_shape=out_shape,
        in_specs=[SMEM] + [HBM] * len(operands),
        out_specs=[HBM] * len(out_shape),
        scratch_shapes=scratch,
        compiler_params=pltpu.CompilerParams(vmem_limit_bytes=SEND_LIMIT) if taken else None,
    )(routes, *operands)


def table_kernel(plan, routes, *refs):
    maps, starts = refs[:-1], refs[-1]
    chips = plan.chips
    section = lax.axis_index("section")
    peer = lax.axis_index("peer")
    chip = lax.div(peer, 2)
    core = lax.rem(peer, 2)
    earlier = lax.rem(section + plan.sections - 1, plan.sections)
    total = jnp.int32(0)
    for p in range(plan.peers):
        starts[p] = total
        total = total + routes[earlier, p, peer]
    spans = plan.sets + ([plan.extra] if plan.spill else [])
    fits = jnp.bool_(True)
    if plan.spill:

        def enough(s, fits):
            for z in range(chips):
                for c in range(chips):
                    one, two = (
                        routes[s, 2 * z + lane, 2 * c] + routes[s, 2 * z + lane, 2 * c + 1]
                        for lane in range(2)
                    )
                    over = jnp.maximum(one, two) - plan.sent
                    level = jnp.logical_and(one + two <= 2 * plan.sent, over <= plan.spill)
                    fits = jnp.logical_and(fits, jnp.logical_or(over <= 0, level))
            return fits

        fits = lax.fori_loop(0, plan.sections, enough, fits)
        maps[-1][0] = fits.astype(jnp.int32)

    def place(sender, position, usable):
        zero = routes[earlier, sender, 2 * chip]
        one = routes[earlier, sender, 2 * chip + 1]
        low = jnp.where(core == 1, zero, 0)
        high = jnp.where(core == 1, zero + one, zero)
        mine = jnp.logical_and(position >= low, position < high)
        return jnp.where(jnp.logical_and(mine, usable), starts[sender] + position - low, -1)

    for (a, b), out in zip(spans, maps):
        for lane in range(2):
            for e in range(chips):
                sender = 2 * (chip ^ e) + (core ^ lane)
                load = routes[earlier, sender, 2 * chip] + routes[earlier, sender, 2 * chip + 1]
                for u in range(a, b):
                    slot = place(sender, u, True)
                    item = plan.sent - 1 - u
                    if 0 <= item < plan.spill:
                        usable = jnp.logical_and(fits, u >= load)
                        other = place(sender ^ 1, plan.sent + item, usable)
                        slot = jnp.maximum(slot, other)
                    out[(lane * chips + e) * (b - a) + u - a] = slot


def run_tables(plan, routes):
    spans = plan.sets + ([plan.extra] if plan.spill else [])
    sizes = [2 * plan.chips * (b - a) for a, b in spans] + [1] * bool(plan.spill)
    return pl.pallas_call(
        functools.partial(table_kernel, plan),
        out_shape=[jax.ShapeDtypeStruct((n,), jnp.int32) for n in sizes],
        in_specs=[SMEM],
        out_specs=[SMEM] * len(sizes),
        scratch_shapes=[pltpu.SMEM((plan.peers,), jnp.int32)],
    )(routes)


def contract_last(left, right):
    return lax.dot_general(
        left, right, (((1,), (1,)), ((), ())), preferred_element_type=jnp.float32
    )


def expand(left, right):
    return jnp.dot(left, right, preferred_element_type=jnp.float32)


def column_block(width):
    for block in (1024, 512, 256, 128):
        if width % block == 0:
            return block
    return width


def prepare_kernel(rank, group, returned, *refs):
    quarters, refs = refs[:4], refs[4:]
    rows_out, w, back = refs[:3]
    g_buf, w_buf, sem = refs[3:]
    capacity, _, width = g_buf.shape
    block = column_block(width)
    blocks = [slice(c * block, (c + 1) * block) for c in range(width // block)]
    peer = lax.axis_index("peer")
    parity, half = lax.rem(peer, 2), lax.rem(lax.div(peer, 2), 2)
    copies = [pltpu.make_async_copy(returned, g_buf, sem.at[4])]
    for i, quarter in enumerate(quarters):
        target = w_buf.at[parity ^ (i // 2), half ^ (i % 2)]
        copies.append(pltpu.make_async_copy(quarter, target, sem.at[i]))
    for copy in copies:
        copy.start()
    for copy in copies:
        copy.wait()
    for tensor in range(2):
        for c in blocks:
            value = w_buf[tensor, :, :, :, c].astype(jnp.float32)
            w[tensor, :, :, c] = value.reshape(-1, rank, block).astype(BF16)
    rows = group * MB

    @pl.loop(0, capacity // group)
    def _(i):
        k = pl.ds(i * group, group)
        r = pl.ds(pl.multiple_of(i * rows, rows), rows)
        total = jnp.zeros((rows, rank), jnp.float32)
        for c in blocks:
            g = g_buf[k, :, c].astype(jnp.float32).reshape(rows, block).astype(BF16)
            rows_out[r, c] = g
            total = total + contract_last(g, w[1, 1, :, c])
        back[r, :] = total.astype(BF16)


def run_prepare(rank, group, returned, quarters):
    capacity, _, width = returned.shape
    vmem = pl.BlockSpec(memory_space=pltpu.VMEM)
    layers = quarters[0].shape[0] * 2 * MB // rank
    return pl.pallas_call(
        functools.partial(prepare_kernel, rank, group),
        out_shape=[
            jax.ShapeDtypeStruct((capacity * MB, width), BF16),
            jax.ShapeDtypeStruct((2, layers, rank, width), BF16),
            jax.ShapeDtypeStruct((capacity * MB, rank), BF16),
        ],
        in_specs=[HBM] * 5,
        out_specs=[vmem] * 3,
        scratch_shapes=[
            pltpu.VMEM((capacity, MB, width), BF16),
            pltpu.VMEM((2, 2, *quarters[0].shape), BF16),
            pltpu.SemaphoreType.DMA((5,)),
        ],
        compiler_params=pltpu.CompilerParams(vmem_limit_bytes=PREPARE_LIMIT),
    )(returned, *quarters)


def step_kernel(plan, rank, group, counts, first, *refs):
    tables, refs = refs[: len(counts)], refs[len(counts) :]
    sources, refs = refs[: sum(counts)], refs[sum(counts) :]
    g_rows, w, back1_rows = refs[:3]
    refs = refs[3:] if first else refs[4:]
    handed, keep, give = refs[:3]
    x_buf, out_buf, xb, hb, g1, h1, small, sem, out_sem, held = refs[3:]
    capacity, _, width = x_buf.shape
    block = column_block(width)
    blocks = [slice(c * block, (c + 1) * block) for c in range(width // block)]
    peer = lax.axis_index("peer")
    parity = lax.rem(peer, 2)
    for k in range(capacity):
        held[k] = 0
    i = 0
    for count, table in zip(counts, tables):
        for j in range(count):
            source = sources[i + j]
            for u in range(source.shape[0]):
                k = table[j * source.shape[0] + u]

                @pl.when(k >= 0)
                def _():
                    held[k] = 1
                    pltpu.make_async_copy(source.at[u], x_buf.at[k], sem.at[k]).start()

        i += count

    @pl.loop(0, capacity)
    def _(k):
        @pl.when(held[k] == 0)
        def _():
            x_buf[k] = jnp.zeros((MB, width), BF16)

    rows = group * MB

    def mean_of(part):
        return jnp.sum(part, axis=-1, keepdims=True) / width

    def lane_sum(value):
        part = value[:, :128]
        for c in range(1, value.shape[1] // 128):
            part = part + value[:, c * 128 : (c + 1) * 128]
        return part

    def send_out(k):
        return pltpu.make_async_copy(out_buf.at[k], handed.at[k], out_sem.at[k])

    def each_sent(k, action):
        if first:
            action()
        else:
            pl.when(held[k] == 1)(action)

    def work(i):
        k = pl.ds(i * group, group)
        r = pl.ds(pl.multiple_of(i * rows, rows), rows)

        @pl.loop(i * group, (i + 1) * group)
        def _(j):
            @pl.when(held[j] == 1)
            def _():
                pltpu.make_async_copy(sources[0].at[0], x_buf.at[j], sem.at[j]).wait()

        part = jnp.zeros((rows, 128), jnp.float32)
        for c in blocks:
            x = x_buf[k, :, c].astype(jnp.float32).reshape(rows, block)
            part = part + lane_sum(x * x)
            xb[r, c] = x.astype(BF16)
        low0 = contract_last(xb[r, :], w[0, 0])
        scale0 = lax.rsqrt(mean_of(part) + EPSILON)
        low0 = (low0 * scale0).astype(BF16)
        part = jnp.zeros((rows, 128), jnp.float32)
        for c in blocks:
            hidden = xb[r, c].astype(jnp.float32) + expand(low0, w[1, 0, :, c])
            h1[:, c] = hidden
            part = part + lane_sum(hidden * hidden)
            hb[r, c] = hidden.astype(BF16)
        low1 = contract_last(hb[r, :], w[0, 1])
        scale1 = lax.rsqrt(mean_of(part) + EPSILON)
        low1 = low1 * scale1
        back1 = back1_rows[r, :]
        mean = jnp.sum(back1.astype(jnp.float32) * low1, axis=-1, keepdims=True) / width
        pull = scale1 * scale1 * mean
        low1 = low1.astype(BF16)
        for c in blocks:
            hidden = h1[:, c]
            out = hidden + expand(low1, w[1, 1, :, c])
            out_buf[k, :, c] = out.reshape(group, MB, block).astype(BF16)
            grad = g_rows[r, c].astype(jnp.float32) + (
                scale1 * expand(back1, w[0, 1, :, c]) - hidden * pull
            )
            g1[r, c] = grad.astype(BF16)
        back0 = contract_last(g1[r, :], w[1, 0])

        @pl.loop(i * group, (i + 1) * group)
        def _(j):
            each_sent(j, lambda: send_out(j).start())

        small[0, r, :] = back0.astype(BF16).astype(jnp.float32) * scale0
        small[1, r, :] = back1.astype(jnp.float32) * scale1
        small[2, r, :] = low0.astype(jnp.float32)
        small[3, r, :] = low1.astype(jnp.float32)

    def rest(i):
        r = pl.ds(pl.multiple_of(i * rows, rows), rows)
        for buffer in (xb, hb, g1):
            buffer[r, :] = jnp.zeros((rows, width), BF16)
        small[:, r, :] = jnp.zeros((4, rows, rank), jnp.float32)

    @pl.loop(0, capacity // group)
    def _(i):
        if first:
            work(i)
        else:
            busy = functools.reduce(jnp.maximum, [held[i * group + j] for j in range(group)])
            pl.when(busy == 1)(lambda: work(i))
            pl.when(busy == 0)(lambda: rest(i))

    sides = [small[l].T.astype(BF16) for l in range(4)]
    others = (xb, hb, g1, g_rows)
    part_width = width // plan.peers
    for z in range(plan.chips):
        for l in range(4):
            at = slice(l * rank, (l + 1) * rank)
            both = expand(sides[l], others[l][:, 2 * z * part_width : 2 * (z + 1) * part_width])
            even, odd = both[:, :part_width], both[:, part_width:]
            keep[z, at, :] = jnp.where(parity == 0, even, odd)
            give[z, at, :] = jnp.where(parity == 0, odd, even).astype(BF16)

    @pl.loop(0, capacity)
    def _(k):
        each_sent(k, lambda: send_out(k).wait())


def run_step(plan, rank, group, tables, sources, prepared, handed=None):
    g_rows = prepared[0]
    rows, width = g_rows.shape
    capacity = plan.capacity
    first = handed is None
    part = (plan.chips, 4 * rank, width // plan.peers)
    vmem = pl.BlockSpec(memory_space=pltpu.VMEM)
    counts = [len(arrays) for arrays in sources]
    flat = [array for arrays in sources for array in arrays]
    carried = () if first else (handed,)
    operands = [*tables, *flat, *prepared, *carried]
    return pl.pallas_call(
        functools.partial(step_kernel, plan, rank, group, counts, first),
        out_shape=[
            jax.ShapeDtypeStruct((capacity, MB, width), BF16),
            jax.ShapeDtypeStruct(part, jnp.float32),
            jax.ShapeDtypeStruct(part, BF16),
        ],
        in_specs=[SMEM] * len(tables) + [HBM] * len(flat) + [vmem] * 3 + [HBM] * len(carried),
        out_specs=[HBM, vmem, vmem],
        input_output_aliases={} if first else {len(operands) - 1: 0},
        scratch_shapes=[
            pltpu.VMEM((capacity, MB, width), BF16),
            pltpu.VMEM((capacity, MB, width), BF16),
            pltpu.VMEM((rows, width), BF16),
            pltpu.VMEM((rows, width), BF16),
            pltpu.VMEM((rows, width), BF16),
            pltpu.VMEM((group * MB, width), jnp.float32),
            pltpu.VMEM((4, rows, rank), jnp.float32),
            pltpu.SemaphoreType.DMA((capacity,)),
            pltpu.SemaphoreType.DMA((capacity,)),
            pltpu.SMEM((capacity,), jnp.int32),
        ],
        compiler_params=pltpu.CompilerParams(vmem_limit_bytes=VMEM_LIMIT),
        cost_estimate=pl.CostEstimate(
            flops=22 * rows * width * rank, bytes_accessed=6 * rows * width, transcendentals=0
        ),
    )(*operands)


def pair_kernel(chips, *refs):
    parts, outs = refs[:-chips], refs[-chips:]
    half = lax.div(lax.axis_index("peer"), 2)
    for e in range(chips):
        z = half ^ e
        total = parts[0][z]
        for part in parts[1:]:
            total = total + part[z].astype(jnp.float32)
        outs[e][...] = total.astype(outs[e].dtype)


def exchange(plan, buffers):
    arrived = [None] * plan.chips
    for e in reversed(range(plan.chips)):
        arrived[e] = lax.ppermute(buffers[e], ("section", "peer"), hop_pairs(plan, 1, 2 * e))
    return arrived


def shards(inbox, routes, adapter_in, adapter_out, returned):
    peers = lax.axis_size("peer")
    sections = lax.axis_size("section")
    tokens, width = inbox.shape[2:]
    layers, rank = adapter_in.shape[1:3]
    micro = tokens // MB
    capacity = returned.shape[2] // MB
    plan = Plan(sections, peers, micro, capacity)
    chips = plan.chips
    axes = ("section", "peer")
    blocks = inbox[0, 0].reshape(micro, MB, width)
    cotangents = returned[0, 0].reshape(capacity, MB, width)

    def share(arrays):
        other = []
        for array in arrays:
            other.append(to_sibling(plan, array))
        return [*arrays, *other]

    halves = [
        weight[0].reshape(layers * rank // MB, MB, width) for weight in (adapter_in, adapter_out)
    ]
    spilling = plan.spill > 0
    sent = run_send(plan, (0, 0), routes, blocks, halves, spilling)
    w_own = lax.ppermute(sent[0], axes, hop_pairs(plan, 1, 0))
    spilled = to_sibling(plan, sent[1]) if spilling else None
    sent = run_send(plan, plan.sets[0], routes, blocks)
    early = exchange(plan, sent)
    tables = run_tables(plan, routes)
    sent = run_send(plan, plan.sets[1], routes, blocks, spilled=spilled)
    late = exchange(plan, sent)
    w_near = lax.ppermute(w_own, "peer", [(p, p ^ 2) for p in range(peers)])
    weights = (w_own, w_near, to_sibling(plan, w_own), to_sibling(plan, w_near))
    group = max(1, capacity // 2)
    prepared = run_prepare(rank, group, cotangents, weights)
    small_group = 4 if capacity % 4 == 0 else 1

    def step_more(table, sources, handed):
        return run_step(plan, rank, small_group, [table], [sources], prepared, handed)

    shared = share(early)
    handed, keep, give = run_step(plan, rank, group, tables[:1], [shared], prepared)
    parts = [keep, to_sibling(plan, give)]
    if spilling:

        def direct(handed, keep):
            extra = exchange(plan, run_send(plan, plan.extra, routes, blocks))
            handed, more, gift = step_more(tables[2], share(extra), handed)
            return handed, keep + more + to_sibling(plan, gift).astype(jnp.float32)

        handed, parts[0] = lax.cond(
            tables[3][0] == 1, lambda *kept: kept, direct, handed, parts[0]
        )
    handed, keep, give = step_more(tables[1], share(late), handed)
    parts += [keep, to_sibling(plan, give)]
    part_width = width // peers
    vmem = pl.BlockSpec(memory_space=pltpu.VMEM)
    summed = pl.pallas_call(
        functools.partial(pair_kernel, chips),
        out_shape=[jax.ShapeDtypeStruct((4 * rank, part_width), BF16)] * chips,
        in_specs=[vmem] * len(parts),
        out_specs=[vmem] * chips,
        compiler_params=pltpu.CompilerParams(vmem_limit_bytes=VMEM_LIMIT),
    )(*parts)
    pieces = [
        lax.ppermute(summed[e], axes, hop_pairs(plan, -1, 2 * e)) for e in reversed(range(chips))
    ]
    mean = functools.reduce(jnp.add, [piece.astype(jnp.float32) for piece in pieces]) / peers
    mean = mean.reshape(2, 1, layers, rank, part_width)
    return (handed.reshape(1, 1, capacity * MB, width), mean[0], mean[1])


def solution(mesh):
    return jax.shard_map(
        shards,
        mesh=mesh,
        in_specs=(
            P("section", "peer", None, None),
            P(),
            P("section", None, None, None),
            P("section", None, None, None),
            P("section", "peer", None, None),
        ),
        out_specs=(
            P("section", "peer", None, None),
            P("section", None, None, "peer"),
            P("section", None, None, "peer"),
        ),
        check_vma=False,
    )
```

time: 219 us -> 119 us (0.54)
  waiting for transfers between devices: 118 us -> 48.9 us
  Pallas kernels: 0 us -> 29.2 us
  local copies, waits for them, and re-layouts: 33.7 us -> 4.78 us
  matrix products: 28.9 us -> 0 us
  starting transfers between devices: 15.1 us -> 34.2 us
  between operations: 14.2 us -> 1.5 us
  other arithmetic: 7.55 us -> 0.05 us
    all_to_all x2 -> x0, waiting for transfers between devices: 68.9 us -> none  [the longest x1 51.2 us: route_backward(): lax.all_to_all(spread_out, 'peer', split_axis=0, concat_axis=0, tiled=True)]
    unnamed x4 -> x0, waiting for transfers between devices: 30.8 us -> none
    ppermute x2 -> x27, waiting for transfers between devices: 18.5 us -> 48.9 us  [the longest x8 35 us: exchange(): lax.ppermute(buffers[e], ('section', 'peer'), hop_pairs(plan, 1, 2 * e))]
    ppermute x2 -> x27, starting transfers between devices: 3.93 us -> 34.2 us  [the longest x8 18.2 us: exchange(): lax.ppermute(buffers[e], ('section', 'peer'), hop_pairs(plan, 1, 2 * e))]
    pallas_call x0 -> x8, Pallas kernels: none -> 29.2 us  [the longest x2 14.8 us: run_step(): pl.pallas_call(functools.partial(step_kernel, plan, rank, group, counts,...]
    dot_general x14 -> x0, matrix products: 28.9 us -> none  [the longest x4 7.54 us: contract_first(): lax.dot_general(left, right, (((0,), (0,)), ((), ())), preferred_element_...]
    unnamed x24 -> x22, local copies, waits for them, and re-layouts: 22 us -> 4.11 us
    all_to_all x2 -> x0, starting transfers between devices: 10.9 us -> none  [the longest x1 6.49 us: route_backward(): lax.all_to_all(spread_out, 'peer', split_axis=0, concat_axis=0, tiled=True)]
  transfers between devices with their start and end apart: 6 -> 27, of which waited for: 4 -> 11; matrix products, arithmetic and copies ran while one was open for 27% -> 0% of each run, Pallas kernels for 0% -> 19%
where the time goes in v1:
time: 119 us
  waiting for transfers between devices  48.9 us (41%)
  starting transfers between devices  34.2 us (29%)
  Pallas kernels  29.2 us (25%)
  local copies, waits for them, and re-layouts  4.78 us (4%)
  between operations  1.5 us (1%)
    ppermute x8, waiting for transfers between devices, exchange(): lax.ppermute(buffers[e], ('section', 'peer'), hop_pairs(plan, 1, 2 * e))  35 us
    ppermute x8, starting transfers between devices, exchange(): lax.ppermute(buffers[e], ('section', 'peer'), hop_pairs(plan, 1, 2 * e))  18.2 us
    pallas_call x2, Pallas kernels, run_step(): pl.pallas_call(functools.partial(step_kernel, plan, rank, group, counts,...  14.8 us
    ppermute x4, starting transfers between devices, shards(): lax.ppermute(summed[e], axes, hop_pairs(plan, -1, 2 * e))  9.18 us
    pallas_call x3, Pallas kernels, run_send(): pl.pallas_call(functools.partial(send_kernel, plan, span, bool(weights),...  9.11 us
    ppermute x4, waiting for transfers between devices, shards(): lax.ppermute(summed[e], axes, hop_pairs(plan, -1, 2 * e))  5.46 us
    ppermute x1, waiting for transfers between devices, shards(): w_own = lax.ppermute(sent[0], axes, hop_pairs(plan, 1, 0))  5.36 us
    unnamed x22, local copies, waits for them, and re-layouts  4.11 us
  transfers between devices with their start and end apart: 27, of which 11 were waited for; matrix products, arithmetic and copies ran while one was open for 0% of the time, Pallas kernels for 19%

profile of v1, /device:TPU:0, one launch (start us, length us, event | category | flops | bytes accessed | tf_op | source)
XLA Modules:
  0.0 118.7 jit_solution(13728794837968993488)
XLA Ops:
  0.7 3.3 %shard_map.77 = (bf16[2,8,5120]{2,1,0:T(8,128)(2,1)}, bf16[4,2,8,5120]{3,2,1,0:T(8,128)(2,1)}) custom-call(s32[4,8,8]{2,1,0:T(8,128)} %routes.7, bf16[16,8,5120]{2,1,0:T(8,128)(2,1)} %bitcast.inbox, bf16[4,8,5120]{2,1,0:T(8,128)(2,1)} %bitcast.10, bf16[4,8,5120]{2,1,0:T(8,128)(2,1)} %bitcast.11), custom_call_target="tpu_custom_call" | custom-call | tf_op jit(solution)/shard_map/pallas_call | solution.py:154
  4.0 3.0 %collective-permute-start.18 = (bf16[2,8,5120]{2,1,0:T(8,128)(2,1)}, bf16[2,8,5120]{2,1,0:T(8,128)(2,1)S(1)}, u32[]{:S(2)}, u32[]{:S(2)}) collective-permute-start(bf16[2,8,5120]{2,1,0:T(8,128)(2,1)} %get-tuple-element.73), channel_id=1, source_target_pairs={{0,8},{1,9},{2,10},{3,11},{4,12},{5,13},{6,14},{7,15},{8,16},{9,17... | collective-permute-start | bytes 491528 | tf_op jit(solution)/shard_map/ppermute | solution.py:521
  7.0 5.4 %collective-permute-done.18.refs_0_ = bf16[2,8,5120]{2,1,0:T(8,128)(2,1)S(1)} collective-permute-done((bf16[2,8,5120]{2,1,0:T(8,128)(2,1)}, bf16[2,8,5120]{2,1,0:T(8,128)(2,1)S(1)}, u32[]{:S(2)}, u32[]{:S(2)}) %collective-permute-start.18) | collective-permute-done | bytes 163872 | tf_op jit(solution)/shard_map/ppermute | solution.py:521
  12.4 1.8 %collective-permute-start.19 = (bf16[2,8,5120]{2,1,0:T(8,128)(2,1)S(1)}, bf16[2,8,5120]{2,1,0:T(8,128)(2,1)S(1)}, u32[]{:S(2)}, u32[]{:S(2)}) collective-permute-start(bf16[2,8,5120]{2,1,0:T(8,128)(2,1)S(1)} %collective-permute-done.18.refs_0_), channel_id=1, source_target_pairs={{0,2},{1,3},{2,0},{3,1},{4,6},{5,7},{6,4},{7,5},{8,10},{9,11},{10,... | collective-permute-start | bytes 491528 | tf_op jit(solution)/shard_map/ppermute | solution.py:528
  14.1 3.1 %shard_map.80 = (bf16[4,8,5120]{2,1,0:T(8,128)(2,1)}, bf16[4,8,5120]{2,1,0:T(8,128)(2,1)}, bf16[4,8,5120]{2,1,0:T(8,128)(2,1)}, bf16[4,8,5120]{2,1,0:T(8,128)(2,1)}) custom-call(s32[4,8,8]{2,1,0:T(8,128)S(1)} %copy-done.10, bf16[16,8,5120]{2,1,0:T(8,128)(2,1)} %bitcast.inbox), custom_call_target="tpu_custom_call" | custom-call | tf_op jit(solution)/shard_map/pallas_call | solution.py:154
  17.3 0.6 collective-permute-start.22
  17.9 2.3 %collective-permute-start.23 = (bf16[4,8,5120]{2,1,0:T(8,128)(2,1)}, bf16[4,8,5120]{2,1,0:T(8,128)(2,1)S(1)}, u32[]{:S(2)}, u32[]{:S(2)}) collective-permute-start(bf16[4,8,5120]{2,1,0:T(8,128)(2,1)} %get-tuple-element.81), channel_id=1, source_target_pairs={{0,10},{1,11},{2,8},{3,9},{4,14},{5,15},{6,12},{7,13},{8,18},{9,19... | collective-permute-start | bytes 983048 | tf_op jit(solution)/shard_map/ppermute | solution.py:493
  20.2 2.6 %collective-permute-start.24 = (bf16[4,8,5120]{2,1,0:T(8,128)(2,1)}, bf16[4,8,5120]{2,1,0:T(8,128)(2,1)S(1)}, u32[]{:S(2)}, u32[]{:S(2)}) collective-permute-start(bf16[4,8,5120]{2,1,0:T(8,128)(2,1)} %get-tuple-element.82), channel_id=1, source_target_pairs={{0,12},{1,13},{2,14},{3,15},{4,8},{5,9},{6,10},{7,11},{8,20},{9,21... | collective-permute-start | bytes 983048 | tf_op jit(solution)/shard_map/ppermute | solution.py:493
  22.8 2.2 %collective-permute-start.25 = (bf16[4,8,5120]{2,1,0:T(8,128)(2,1)}, bf16[4,8,5120]{2,1,0:T(8,128)(2,1)}, u32[]{:S(2)}, u32[]{:S(2)}) collective-permute-start(bf16[4,8,5120]{2,1,0:T(8,128)(2,1)} %get-tuple-element.83), channel_id=1, source_target_pairs={{0,14},{1,15},{2,12},{3,13},{4,10},{5,11},{6,8},{7,9},{8,22},{9,23... | collective-permute-start | bytes 983048 | tf_op jit(solution)/shard_map/ppermute | solution.py:493
  25.0 0.7 copy-done.3
  25.7 22.1 %collective-permute-done.22.refs_1_ = bf16[4,8,5120]{2,1,0:T(8,128)(2,1)S(1)} collective-permute-done((bf16[4,8,5120]{2,1,0:T(8,128)(2,1)}, bf16[4,8,5120]{2,1,0:T(8,128)(2,1)S(1)}, u32[]{:S(2)}, u32[]{:S(2)}) %collective-permute-start.22) | collective-permute-done | bytes 327712 | tf_op jit(solution)/shard_map/ppermute | solution.py:493
  47.8 0.5 collective-permute-start.26
  48.3 0.1 collective-permute-start.27
  48.4 0.4 collective-permute-start.28
  48.8 0.6 collective-permute-done.21.refs_3_
  49.4 0.7 copy-done.5
  50.1 0.1 collective-permute-start.29
  50.2 2.2 %shard_map.76 = (s32[32]{0:T(128)}, s32[16]{0:T(128)}, s32[16]{0:T(128)S(1)}, s32[1]{0:T(128)}) custom-call(s32[4,8,8]{2,1,0:T(8,128)S(1)} %copy-done.10), custom_call_target="tpu_custom_call" | custom-call | tf_op jit(solution)/shard_map/pallas_call | solution.py:221
  52.5 0.0 copy-start.7
  53.2 0.9 copy-done.2
  54.1 0.9 copy-done.4
  55.0 0.9 copy-done.6
  55.9 3.0 %shard_map.79 = (bf16[160,5120]{1,0:T(8,128)(2,1)}, bf16[2,2,16,5120]{3,2,1,0:T(8,128)(2,1)}, bf16[160,16]{1,0:T(8,128)(2,1)S(1)}) custom-call(bf16[20,8,5120]{2,1,0:T(8,128)(2,1)S(1)} %bitcast.8, bf16[2,8,5120]{2,1,0:T(8,128)(2,1)S(1)} %collective-permute-done.18.refs_0_, bf16[2,8,5120]{2,1,0:T(8,128)(2,1)S(1)} %copy-done.2, ...), custom_call_target="tpu_custom_call" | custom-call | tf_op jit(solution)/shard_map/pallas_call | solution.py:286
  58.9 10.7 %shard_map.81 = (bf16[20,8,5120]{2,1,0:T(8,128)(2,1)}, f32[4,64,640]{2,1,0:T(8,128)}, bf16[4,64,640]{2,1,0:T(8,128)(2,1)S(1)}) custom-call(s32[32]{0:T(128)S(1)} %copy-done.7, bf16[4,8,5120]{2,1,0:T(8,128)(2,1)S(1)} %collective-permute-done.22.refs_1_, bf16[4,8,5120]{2,1,0:T(8,128)(2,1)S(1)} %collective-permute-done.23.refs_2_, ...), custom_call_target="tpu_custom_call" | custom-call | flops 288358400 | bytes 4915200 | tf_op jit(solution)/shard_map/pallas_call | solution.py:450
  69.7 2.7 %shard_map.78 = (bf16[2,8,5120]{2,1,0:T(8,128)(2,1)S(1)}, bf16[2,8,5120]{2,1,0:T(8,128)(2,1)S(1)}, bf16[2,8,5120]{2,1,0:T(8,128)(2,1)S(1)}, bf16[2,8,5120]{2,1,0:T(8,128)(2,1)S(1)}) custom-call(s32[4,8,8]{2,1,0:T(8,128)S(1)} %copy-done.10, bf16[16,8,5120]{2,1,0:T(8,128)(2,1)} %bitcast.inbox, bf16[4,2,8,5120]{3,2,1,0:T(8,128)(2,1)S(1)} %collective-permute-done.9.refs_0_), custom_call_target="tpu_custom_call" | custom-call | tf_op jit(solution)/shard_map/pallas_call | solution.py:154
  72.3 0.1 collective-permute-start.10
  72.4 0.0 copy-start.8
  72.5 6.9 %collective-permute-start.11 = (bf16[2,8,5120]{2,1,0:T(8,128)(2,1)S(1)}, bf16[2,8,5120]{2,1,0:T(8,128)(2,1)S(1)}, u32[]{:S(2)}, u32[]{:S(2)}) collective-permute-start(bf16[2,8,5120]{2,1,0:T(8,128)(2,1)S(1)} %get-tuple-element.70), channel_id=1, source_target_pairs={{0,10},{1,11},{2,8},{3,9},{4,14},{5,15},{6,12},{7,13},{8,18},{9,19... | collective-permute-start | bytes 491528 | tf_op jit(solution)/shard_map/ppermute | solution.py:493
  79.4 2.6 %collective-permute-start.12 = (bf16[2,8,5120]{2,1,0:T(8,128)(2,1)S(1)}, bf16[2,8,5120]{2,1,0:T(8,128)(2,1)S(1)}, u32[]{:S(2)}, u32[]{:S(2)}) collective-permute-start(bf16[2,8,5120]{2,1,0:T(8,128)(2,1)S(1)} %get-tuple-element.71), channel_id=1, source_target_pairs={{0,12},{1,13},{2,14},{3,15},{4,8},{5,9},{6,10},{7,11},{8,20},{9,21... | collective-permute-start | bytes 491528 | tf_op jit(solution)/shard_map/ppermute | solution.py:493
  82.0 0.9 collective-permute-start.13
  82.9 4.5 %collective-permute-done.11.refs_2_ = bf16[2,8,5120]{2,1,0:T(8,128)(2,1)S(1)} collective-permute-done((bf16[2,8,5120]{2,1,0:T(8,128)(2,1)S(1)}, bf16[2,8,5120]{2,1,0:T(8,128)(2,1)S(1)}, u32[]{:S(2)}, u32[]{:S(2)}) %collective-permute-start.11) | collective-permute-done | bytes 163872 | tf_op jit(solution)/shard_map/ppermute | solution.py:493
  87.4 8.4 %collective-permute-done.12.refs_3_ = bf16[2,8,5120]{2,1,0:T(8,128)(2,1)S(1)} collective-permute-done((bf16[2,8,5120]{2,1,0:T(8,128)(2,1)S(1)}, bf16[2,8,5120]{2,1,0:T(8,128)(2,1)S(1)}, u32[]{:S(2)}, u32[]{:S(2)}) %collective-permute-start.12) | collective-permute-done | bytes 163872 | tf_op jit(solution)/shard_map/ppermute | solution.py:493
  95.8 0.5 collective-permute-start.17
  96.3 0.0 collective-permute-start.30
  96.3 0.9 collective-permute-done.16.refs_7_
  97.2 0.2 collective-permute-done.17.refs_8_
  97.4 4.0 %shard_map.82 = (bf16[20,8,5120]{2,1,0:T(8,128)(2,1)}, f32[4,64,640]{2,1,0:T(8,128)S(1)}, bf16[4,64,640]{2,1,0:T(8,128)(2,1)S(1)}) custom-call(s32[16]{0:T(128)S(1)} %copy-done.8, bf16[2,8,5120]{2,1,0:T(8,128)(2,1)S(1)} %collective-permute-done.10.refs_1_, bf16[2,8,5120]{2,1,0:T(8,128)(2,1)S(1)} %collective-permute-done.11.refs_2_, ...), custom_call_target="tpu_custom_call", output_to_operand_aliasing={{0}: (12, {})} | custom-call | flops 288358400 | bytes 4915200 | tf_op jit(solution)/shard_map/pallas_call | solution.py:450
  101.5 0.3 collective-permute-start.31
  101.8 1.3 %collective-permute-done.31.refs_3_ = bf16[4,64,640]{2,1,0:T(8,128)(2,1)S(1)} collective-permute-done((bf16[4,64,640]{2,1,0:T(8,128)(2,1)S(1)}, bf16[4,64,640]{2,1,0:T(8,128)(2,1)S(1)}, u32[]{:S(2)}, u32[]{:S(2)}) %collective-permute-start.31) | collective-permute-done | bytes 327712 | tf_op jit(solution)/shard_map/ppermute | solution.py:44
  103.2 0.2 shard_map.83
  103.3 3.4 %collective-permute-start.32 = (bf16[64,640]{1,0:T(8,128)(2,1)S(1)}, bf16[64,640]{1,0:T(8,128)(2,1)S(1)}, u32[]{:S(2)}, u32[]{:S(2)}) collective-permute-start(bf16[64,640]{1,0:T(8,128)(2,1)S(1)} %get-tuple-element.92), channel_id=1, source_target_pairs={{0,30},{1,31},{2,28},{3,29},{4,26},{5,27},{6,24},{7,25},{8,6},{9,7... | collective-permute-start | bytes 245768 | tf_op jit(solution)/shard_map/ppermute | solution.py:562
  106.8 2.9 %collective-permute-start.33 = (bf16[64,640]{1,0:T(8,128)(2,1)S(1)}, bf16[64,640]{1,0:T(8,128)(2,1)S(1)}, u32[]{:S(2)}, u32[]{:S(2)}) collective-permute-start(bf16[64,640]{1,0:T(8,128)(2,1)S(1)} %get-tuple-element.93), channel_id=1, source_target_pairs={{0,28},{1,29},{2,30},{3,31},{4,24},{5,25},{6,26},{7,27},{8,4},{9,5... | collective-permute-start | bytes 245768 | tf_op jit(solution)/shard_map/ppermute | solution.py:562
  109.7 2.8 %collective-permute-start.34 = (bf16[64,640]{1,0:T(8,128)(2,1)S(1)}, bf16[64,640]{1,0:T(8,128)(2,1)S(1)}, u32[]{:S(2)}, u32[]{:S(2)}) collective-permute-start(bf16[64,640]{1,0:T(8,128)(2,1)S(1)} %get-tuple-element.94), channel_id=1, source_target_pairs={{0,26},{1,27},{2,24},{3,25},{4,30},{5,31},{6,28},{7,29},{8,2},{9,3... | collective-permute-start | bytes 245768 | tf_op jit(solution)/shard_map/ppermute | solution.py:562
  112.5 0.1 collective-permute-start.35
  112.5 3.6 %collective-permute-done.33 = bf16[64,640]{1,0:T(8,128)(2,1)S(1)} collective-permute-done((bf16[64,640]{1,0:T(8,128)(2,1)S(1)}, bf16[64,640]{1,0:T(8,128)(2,1)S(1)}, u32[]{:S(2)}, u32[]{:S(2)}) %collective-permute-start.33) | collective-permute-done | bytes 81952 | tf_op jit(solution)/shard_map/ppermute | solution.py:562
  116.1 0.2 collective-permute-done.34
  116.3 1.7 %collective-permute-done.35 = bf16[64,640]{1,0:T(8,128)(2,1)S(1)} collective-permute-done((bf16[64,640]{1,0:T(8,128)(2,1)S(1)}, bf16[64,640]{1,0:T(8,128)(2,1)S(1)}, u32[]{:S(2)}, u32[]{:S(2)}) %collective-permute-start.35) | collective-permute-done | bytes 81952 | tf_op jit(solution)/shard_map/ppermute | solution.py:562
  118.0 0.7 fusion
  (39 shorter events, 0.1 us)
Async XLA Ops:
  0.6 13.5 %copy-start.10 = (s32[4,8,8]{2,1,0:T(8,128)S(1)}, s32[4,8,8]{2,1,0:T(8,128)}, u32[]{:S(2)}) copy-start(s32[4,8,8]{2,1,0:T(8,128)} %routes.7) | copy-start | bytes 3076
  0.6 52.5 %copy-start = (bf16[1,1,160,5120]{3,2,1,0:T(8,128)(2,1)S(1)}, bf16[1,1,160,5120]{3,2,1,0:T(8,128)(2,1)}, u32[]{:S(2)}) copy-start(bf16[1,1,160,5120]{3,2,1,0:T(8,128)(2,1)} %param.11) | copy-start | bytes 4915204
  4.0 8.4 %collective-permute-start.18 = (bf16[2,8,5120]{2,1,0:T(8,128)(2,1)}, bf16[2,8,5120]{2,1,0:T(8,128)(2,1)S(1)}, u32[]{:S(2)}, u32[]{:S(2)}) collective-permute-start(bf16[2,8,5120]{2,1,0:T(8,128)(2,1)} %get-tuple-element.73), channel_id=1, source_target_pairs={{0,8},{1,9},{2,10},{3,11},{4,12},{5,13},{6,14},{7,15},{8,16},{9,17... | collective-permute-start | bytes 491528 | tf_op jit(solution)/shard_map/ppermute | solution.py:521
  12.4 10.4 %collective-permute-start.19 = (bf16[2,8,5120]{2,1,0:T(8,128)(2,1)S(1)}, bf16[2,8,5120]{2,1,0:T(8,128)(2,1)S(1)}, u32[]{:S(2)}, u32[]{:S(2)}) collective-permute-start(bf16[2,8,5120]{2,1,0:T(8,128)(2,1)S(1)} %collective-permute-done.18.refs_0_), channel_id=1, source_target_pairs={{0,2},{1,3},{2,0},{3,1},{4,6},{5,7},{6,4},{7,5},{8,10},{9,11},{10,... | collective-permute-start | bytes 491528 | tf_op jit(solution)/shard_map/ppermute | solution.py:528
  17.3 30.5 %collective-permute-start.22 = (bf16[4,8,5120]{2,1,0:T(8,128)(2,1)}, bf16[4,8,5120]{2,1,0:T(8,128)(2,1)S(1)}, u32[]{:S(2)}, u32[]{:S(2)}) collective-permute-start(bf16[4,8,5120]{2,1,0:T(8,128)(2,1)} %get-tuple-element.80), channel_id=1, source_target_pairs={{0,8},{1,9},{2,10},{3,11},{4,12},{5,13},{6,14},{7,15},{8,16},{9,17... | collective-permute-start | bytes 983048 | tf_op jit(solution)/shard_map/ppermute | solution.py:493
  17.9 7.1 %collective-permute-start.20 = (bf16[2,8,5120]{2,1,0:T(8,128)(2,1)S(1)}, bf16[2,8,5120]{2,1,0:T(8,128)(2,1)S(1)}, u32[]{:S(2)}, u32[]{:S(2)}) collective-permute-start(bf16[2,8,5120]{2,1,0:T(8,128)(2,1)S(1)} %collective-permute-done.18.refs_0_), channel_id=1, source_target_pairs={{0,1},{1,0},{2,3},{3,2},{4,5},{5,4},{6,7},{7,6},{8,9},{9,8},{10,11... | collective-permute-start | bytes 491528 | tf_op jit(solution)/shard_map/ppermute | solution.py:44
  17.9 29.9 %collective-permute-start.23 = (bf16[4,8,5120]{2,1,0:T(8,128)(2,1)}, bf16[4,8,5120]{2,1,0:T(8,128)(2,1)S(1)}, u32[]{:S(2)}, u32[]{:S(2)}) collective-permute-start(bf16[4,8,5120]{2,1,0:T(8,128)(2,1)} %get-tuple-element.81), channel_id=1, source_target_pairs={{0,10},{1,11},{2,8},{3,9},{4,14},{5,15},{6,12},{7,13},{8,18},{9,19... | collective-permute-start | bytes 983048 | tf_op jit(solution)/shard_map/ppermute | solution.py:493
  20.2 28.1 %collective-permute-start.24 = (bf16[4,8,5120]{2,1,0:T(8,128)(2,1)}, bf16[4,8,5120]{2,1,0:T(8,128)(2,1)S(1)}, u32[]{:S(2)}, u32[]{:S(2)}) collective-permute-start(bf16[4,8,5120]{2,1,0:T(8,128)(2,1)} %get-tuple-element.82), channel_id=1, source_target_pairs={{0,12},{1,13},{2,14},{3,15},{4,8},{5,9},{6,10},{7,11},{8,20},{9,21... | collective-permute-start | bytes 983048 | tf_op jit(solution)/shard_map/ppermute | solution.py:493
  22.8 2.2 %copy-start.1 = (bf16[2,8,5120]{2,1,0:T(8,128)(2,1)}, bf16[2,8,5120]{2,1,0:T(8,128)(2,1)S(1)}, u32[]{:S(2)}) copy-start(bf16[2,8,5120]{2,1,0:T(8,128)(2,1)S(1)} %collective-permute-done.19.refs_1_) | copy-start | bytes 491524
  22.8 25.6 %collective-permute-start.25 = (bf16[4,8,5120]{2,1,0:T(8,128)(2,1)}, bf16[4,8,5120]{2,1,0:T(8,128)(2,1)}, u32[]{:S(2)}, u32[]{:S(2)}) collective-permute-start(bf16[4,8,5120]{2,1,0:T(8,128)(2,1)} %get-tuple-element.83), channel_id=1, source_target_pairs={{0,14},{1,15},{2,12},{3,13},{4,10},{5,11},{6,8},{7,9},{8,22},{9,23... | collective-permute-start | bytes 983048 | tf_op jit(solution)/shard_map/ppermute | solution.py:493
  25.0 0.7 copy-start.3
  25.6 44.0 %collective-permute-start.9 = (bf16[4,2,8,5120]{3,2,1,0:T(8,128)(2,1)}, bf16[4,2,8,5120]{3,2,1,0:T(8,128)(2,1)S(1)}, u32[]{:S(2)}, u32[]{:S(2)}) collective-permute-start(bf16[4,2,8,5120]{3,2,1,0:T(8,128)(2,1)} %get-tuple-element.68), channel_id=1, source_target_pairs={{0,1},{1,0},{2,3},{3,2},{4,5},{5,4},{6,7},{7,6},{8,9},{9,8},{10,11... | collective-permute-start | bytes 1966088 | tf_op jit(solution)/shard_map/ppermute | solution.py:44
  47.8 1.6 %collective-permute-start.21 = (bf16[2,8,5120]{2,1,0:T(8,128)(2,1)}, bf16[2,8,5120]{2,1,0:T(8,128)(2,1)S(1)}, u32[]{:S(2)}, u32[]{:S(2)}) collective-permute-start(bf16[2,8,5120]{2,1,0:T(8,128)(2,1)} %copy-done.1), channel_id=1, source_target_pairs={{0,1},{1,0},{2,3},{3,2},{4,5},{5,4},{6,7},{7,6},{8,9},{9,8},{10,11... | collective-permute-start | bytes 491528 | tf_op jit(solution)/shard_map/ppermute | solution.py:44
  47.8 11.1 %collective-permute-start.26 = (bf16[4,8,5120]{2,1,0:T(8,128)(2,1)S(1)}, bf16[4,8,5120]{2,1,0:T(8,128)(2,1)}, u32[]{:S(2)}, u32[]{:S(2)}) collective-permute-start(bf16[4,8,5120]{2,1,0:T(8,128)(2,1)S(1)} %collective-permute-done.22.refs_1_), channel_id=1, source_target_pairs={{0,1},{1,0},{2,3},{3,2},{4,5},{5,4},{6,7},{7,6},{8,9},{9,8},{10,11... | collective-permute-start | bytes 983048 | tf_op jit(solution)/shard_map/ppermute | solution.py:44
  48.3 10.6 %collective-permute-start.27 = (bf16[4,8,5120]{2,1,0:T(8,128)(2,1)S(1)}, bf16[4,8,5120]{2,1,0:T(8,128)(2,1)}, u32[]{:S(2)}, u32[]{:S(2)}) collective-permute-start(bf16[4,8,5120]{2,1,0:T(8,128)(2,1)S(1)} %collective-permute-done.23.refs_2_), channel_id=1, source_target_pairs={{0,1},{1,0},{2,3},{3,2},{4,5},{5,4},{6,7},{7,6},{8,9},{9,8},{10,11... | collective-permute-start | bytes 983048 | tf_op jit(solution)/shard_map/ppermute | solution.py:44
  48.4 10.5 %collective-permute-start.28 = (bf16[4,8,5120]{2,1,0:T(8,128)(2,1)S(1)}, bf16[4,8,5120]{2,1,0:T(8,128)(2,1)}, u32[]{:S(2)}, u32[]{:S(2)}) collective-permute-start(bf16[4,8,5120]{2,1,0:T(8,128)(2,1)S(1)} %collective-permute-done.24.refs_3_), channel_id=1, source_target_pairs={{0,1},{1,0},{2,3},{3,2},{4,5},{5,4},{6,7},{7,6},{8,9},{9,8},{10,11... | collective-permute-start | bytes 983048 | tf_op jit(solution)/shard_map/ppermute | solution.py:44
  49.4 0.7 copy-start.5
  50.1 8.8 %collective-permute-start.29 = (bf16[4,8,5120]{2,1,0:T(8,128)(2,1)}, bf16[4,8,5120]{2,1,0:T(8,128)(2,1)}, u32[]{:S(2)}, u32[]{:S(2)}) collective-permute-start(bf16[4,8,5120]{2,1,0:T(8,128)(2,1)} %collective-permute-done.25.refs_4_), channel_id=1, source_target_pairs={{0,1},{1,0},{2,3},{3,2},{4,5},{5,4},{6,7},{7,6},{8,9},{9,8},{10,11... | collective-permute-start | bytes 983048 | tf_op jit(solution)/shard_map/ppermute | solution.py:44
  52.5 6.4 %copy-start.7 = (s32[32]{0:T(128)S(1)}, s32[32]{0:T(128)}, u32[]{:S(2)}) copy-start(s32[32]{0:T(128)} %get-tuple-element.79.refs_0_) | copy-start | bytes 388
  53.1 0.9 copy-start.2
  54.1 0.9 copy-start.4
  55.0 0.9 copy-start.6
  69.6 2.8 %copy-start.9 = (f32[4,64,640]{2,1,0:T(8,128)S(1)}, f32[4,64,640]{2,1,0:T(8,128)}, u32[]{:S(2)}) copy-start(f32[4,64,640]{2,1,0:T(8,128)} %get-tuple-element.85) | copy-start | bytes 1966084
  72.3 10.6 %collective-permute-start.10 = (bf16[2,8,5120]{2,1,0:T(8,128)(2,1)S(1)}, bf16[2,8,5120]{2,1,0:T(8,128)(2,1)S(1)}, u32[]{:S(2)}, u32[]{:S(2)}) collective-permute-start(bf16[2,8,5120]{2,1,0:T(8,128)(2,1)S(1)} %get-tuple-element.69), channel_id=1, source_target_pairs={{0,8},{1,9},{2,10},{3,11},{4,12},{5,13},{6,14},{7,15},{8,16},{9,17... | collective-permute-start | bytes 491528 | tf_op jit(solution)/shard_map/ppermute | solution.py:493
  72.4 25.0 %copy-start.8 = (s32[16]{0:T(128)S(1)}, s32[16]{0:T(128)}, u32[]{:S(2)}) copy-start(s32[16]{0:T(128)} %get-tuple-element.67.refs_0_) | copy-start | bytes 196
  72.5 14.9 %collective-permute-start.11 = (bf16[2,8,5120]{2,1,0:T(8,128)(2,1)S(1)}, bf16[2,8,5120]{2,1,0:T(8,128)(2,1)S(1)}, u32[]{:S(2)}, u32[]{:S(2)}) collective-permute-start(bf16[2,8,5120]{2,1,0:T(8,128)(2,1)S(1)} %get-tuple-element.70), channel_id=1, source_target_pairs={{0,10},{1,11},{2,8},{3,9},{4,14},{5,15},{6,12},{7,13},{8,18},{9,19... | collective-permute-start | bytes 491528 | tf_op jit(solution)/shard_map/ppermute | solution.py:493
  79.4 16.4 %collective-permute-start.12 = (bf16[2,8,5120]{2,1,0:T(8,128)(2,1)S(1)}, bf16[2,8,5120]{2,1,0:T(8,128)(2,1)S(1)}, u32[]{:S(2)}, u32[]{:S(2)}) collective-permute-start(bf16[2,8,5120]{2,1,0:T(8,128)(2,1)S(1)} %get-tuple-element.71), channel_id=1, source_target_pairs={{0,12},{1,13},{2,14},{3,15},{4,8},{5,9},{6,10},{7,11},{8,20},{9,21... | collective-permute-start | bytes 491528 | tf_op jit(solution)/shard_map/ppermute | solution.py:493
  82.0 13.9 %collective-permute-start.13 = (bf16[2,8,5120]{2,1,0:T(8,128)(2,1)S(1)}, bf16[2,8,5120]{2,1,0:T(8,128)(2,1)S(1)}, u32[]{:S(2)}, u32[]{:S(2)}) collective-permute-start(bf16[2,8,5120]{2,1,0:T(8,128)(2,1)S(1)} %get-tuple-element.72), channel_id=1, source_target_pairs={{0,14},{1,15},{2,12},{3,13},{4,10},{5,11},{6,8},{7,9},{8,22},{9,23... | collective-permute-start | bytes 491528 | tf_op jit(solution)/shard_map/ppermute | solution.py:493
  82.9 13.4 %collective-permute-start.14 = (bf16[2,8,5120]{2,1,0:T(8,128)(2,1)S(1)}, bf16[2,8,5120]{2,1,0:T(8,128)(2,1)S(1)}, u32[]{:S(2)}, u32[]{:S(2)}) collective-permute-start(bf16[2,8,5120]{2,1,0:T(8,128)(2,1)S(1)} %collective-permute-done.10.refs_1_), channel_id=1, source_target_pairs={{0,1},{1,0},{2,3},{3,2},{4,5},{5,4},{6,7},{7,6},{8,9},{9,8},{10,11... | collective-permute-start | bytes 491528 | tf_op jit(solution)/shard_map/ppermute | solution.py:44
  87.4 8.9 %collective-permute-start.15 = (bf16[2,8,5120]{2,1,0:T(8,128)(2,1)S(1)}, bf16[2,8,5120]{2,1,0:T(8,128)(2,1)S(1)}, u32[]{:S(2)}, u32[]{:S(2)}) collective-permute-start(bf16[2,8,5120]{2,1,0:T(8,128)(2,1)S(1)} %collective-permute-done.11.refs_2_), channel_id=1, source_target_pairs={{0,1},{1,0},{2,3},{3,2},{4,5},{5,4},{6,7},{7,6},{8,9},{9,8},{10,11... | collective-permute-start | bytes 491528 | tf_op jit(solution)/shard_map/ppermute | solution.py:44
  95.8 1.4 %collective-permute-start.16 = (bf16[2,8,5120]{2,1,0:T(8,128)(2,1)S(1)}, bf16[2,8,5120]{2,1,0:T(8,128)(2,1)S(1)}, u32[]{:S(2)}, u32[]{:S(2)}) collective-permute-start(bf16[2,8,5120]{2,1,0:T(8,128)(2,1)S(1)} %collective-permute-done.12.refs_3_), channel_id=1, source_target_pairs={{0,1},{1,0},{2,3},{3,2},{4,5},{5,4},{6,7},{7,6},{8,9},{9,8},{10,11... | collective-permute-start | bytes 491528 | tf_op jit(solution)/shard_map/ppermute | solution.py:44
  95.8 1.6 %collective-permute-start.17 = (bf16[2,8,5120]{2,1,0:T(8,128)(2,1)S(1)}, bf16[2,8,5120]{2,1,0:T(8,128)(2,1)S(1)}, u32[]{:S(2)}, u32[]{:S(2)}) collective-permute-start(bf16[2,8,5120]{2,1,0:T(8,128)(2,1)S(1)} %collective-permute-done.13.refs_4_), channel_id=1, source_target_pairs={{0,1},{1,0},{2,3},{3,2},{4,5},{5,4},{6,7},{7,6},{8,9},{9,8},{10,11... | collective-permute-start | bytes 491528 | tf_op jit(solution)/shard_map/ppermute | solution.py:44
  96.3 5.5 %collective-permute-start.30 = (bf16[4,64,640]{2,1,0:T(8,128)(2,1)S(1)}, bf16[4,64,640]{2,1,0:T(8,128)(2,1)S(1)}, u32[]{:S(2)}, u32[]{:S(2)}) collective-permute-start(bf16[4,64,640]{2,1,0:T(8,128)(2,1)S(1)} %get-tuple-element.89), channel_id=1, source_target_pairs={{0,1},{1,0},{2,3},{3,2},{4,5},{5,4},{6,7},{7,6},{8,9},{9,8},{10,11... | collective-permute-start | bytes 983048 | tf_op jit(solution)/shard_map/ppermute | solution.py:44
  101.5 1.7 %collective-permute-start.31 = (bf16[4,64,640]{2,1,0:T(8,128)(2,1)S(1)}, bf16[4,64,640]{2,1,0:T(8,128)(2,1)S(1)}, u32[]{:S(2)}, u32[]{:S(2)}) collective-permute-start(bf16[4,64,640]{2,1,0:T(8,128)(2,1)S(1)} %get-tuple-element.91), channel_id=1, source_target_pairs={{0,1},{1,0},{2,3},{3,2},{4,5},{5,4},{6,7},{7,6},{8,9},{9,8},{10,11... | collective-permute-start | bytes 983048 | tf_op jit(solution)/shard_map/ppermute | solution.py:44
  103.3 9.2 %collective-permute-start.32 = (bf16[64,640]{1,0:T(8,128)(2,1)S(1)}, bf16[64,640]{1,0:T(8,128)(2,1)S(1)}, u32[]{:S(2)}, u32[]{:S(2)}) collective-permute-start(bf16[64,640]{1,0:T(8,128)(2,1)S(1)} %get-tuple-element.92), channel_id=1, source_target_pairs={{0,30},{1,31},{2,28},{3,29},{4,26},{5,27},{6,24},{7,25},{8,6},{9,7... | collective-permute-start | bytes 245768 | tf_op jit(solution)/shard_map/ppermute | solution.py:562
  106.8 9.3 %collective-permute-start.33 = (bf16[64,640]{1,0:T(8,128)(2,1)S(1)}, bf16[64,640]{1,0:T(8,128)(2,1)S(1)}, u32[]{:S(2)}, u32[]{:S(2)}) collective-permute-start(bf16[64,640]{1,0:T(8,128)(2,1)S(1)} %get-tuple-element.93), channel_id=1, source_target_pairs={{0,28},{1,29},{2,30},{3,31},{4,24},{5,25},{6,26},{7,27},{8,4},{9,5... | collective-permute-start | bytes 245768 | tf_op jit(solution)/shard_map/ppermute | solution.py:562
  109.7 6.6 %collective-permute-start.34 = (bf16[64,640]{1,0:T(8,128)(2,1)S(1)}, bf16[64,640]{1,0:T(8,128)(2,1)S(1)}, u32[]{:S(2)}, u32[]{:S(2)}) collective-permute-start(bf16[64,640]{1,0:T(8,128)(2,1)S(1)} %get-tuple-element.94), channel_id=1, source_target_pairs={{0,26},{1,27},{2,24},{3,25},{4,30},{5,31},{6,28},{7,29},{8,2},{9,3... | collective-permute-start | bytes 245768 | tf_op jit(solution)/shard_map/ppermute | solution.py:562
  112.5 5.5 %collective-permute-start.35 = (bf16[64,640]{1,0:T(8,128)(2,1)S(1)}, bf16[64,640]{1,0:T(8,128)(2,1)S(1)}, u32[]{:S(2)}, u32[]{:S(2)}) collective-permute-start(bf16[64,640]{1,0:T(8,128)(2,1)S(1)} %get-tuple-element.95), channel_id=1, source_target_pairs={{0,24},{1,25},{2,26},{3,27},{4,28},{5,29},{6,30},{7,31},{8,0},{9,1... | collective-permute-start | bytes 245768 | tf_op jit(solution)/shard_map/ppermute | solution.py:562

commit v2 on v1

--- a/solution.py
+++ b/solution.py
@@ -304,10 +304,12 @@
 def step_kernel(plan, rank, group, counts, first, *refs):
     tables, refs = refs[: len(counts)], refs[len(counts) :]
     sources, refs = refs[: sum(counts)], refs[sum(counts) :]
-    g_rows, w, back1_rows = refs[:3]
+    g_source, w, back1_rows = refs[:3]
     refs = refs[3:] if first else refs[4:]
     handed, keep, give = refs[:3]
-    x_buf, out_buf, xb, hb, g1, h1, small, sem, out_sem, held = refs[3:]
+    x_buf, out_buf, xb, hb, g1, h1, small, g_rows, sem, out_sem, g_sem, held, ready = refs[3:]
+    g_copy = pltpu.make_async_copy(g_source, g_rows, g_sem)
+    ready[0] = 0
     capacity, _, width = x_buf.shape
     block = column_block(width)
     blocks = [slice(c * block, (c + 1) * block) for c in range(width // block)]
@@ -331,7 +333,10 @@
 
     @pl.loop(0, capacity)
     def _(k):
-        @pl.when(held[k] == 0)
+        near = k - lax.rem(k, group)
+        busy = functools.reduce(jnp.maximum, [held[near + j] for j in range(group)])
+
+        @pl.when(jnp.logical_and(held[k] == 0, jnp.logical_or(busy == 1, first)))
         def _():
             x_buf[k] = jnp.zeros((MB, width), BF16)
 
@@ -386,6 +391,8 @@
         mean = jnp.sum(back1.astype(jnp.float32) * low1, axis=-1, keepdims=True) / width
         pull = scale1 * scale1 * mean
         low1 = low1.astype(BF16)
+        pl.when(ready[0] == 1)(g_copy.wait)
+        ready[0] = 2
         for c in blocks:
             hidden = h1[:, c]
             out = hidden + expand(low1, w[1, 1, :, c])
@@ -411,6 +418,13 @@
             buffer[r, :] = jnp.zeros((rows, width), BF16)
         small[:, r, :] = jnp.zeros((4, rows, rank), jnp.float32)
 
+    any_held = functools.reduce(jnp.maximum, [held[k] for k in range(capacity)])
+
+    @pl.when(jnp.logical_or(any_held == 1, first))
+    def _():
+        g_copy.start()
+        ready[0] = 1
+
     @pl.loop(0, capacity // group)
     def _(i):
         if first:
@@ -418,18 +432,29 @@
         else:
             busy = functools.reduce(jnp.maximum, [held[i * group + j] for j in range(group)])
             pl.when(busy == 1)(lambda: work(i))
-            pl.when(busy == 0)(lambda: rest(i))
-
-    sides = [small[l].T.astype(BF16) for l in range(4)]
-    others = (xb, hb, g1, g_rows)
-    part_width = width // plan.peers
-    for z in range(plan.chips):
-        for l in range(4):
-            at = slice(l * rank, (l + 1) * rank)
-            both = expand(sides[l], others[l][:, 2 * z * part_width : 2 * (z + 1) * part_width])
-            even, odd = both[:, :part_width], both[:, part_width:]
-            keep[z, at, :] = jnp.where(parity == 0, even, odd)
-            give[z, at, :] = jnp.where(parity == 0, odd, even).astype(BF16)
+            pl.when(jnp.logical_and(busy == 0, any_held == 1))(lambda: rest(i))
+
+    def gather_terms():
+        sides = [small[l].T.astype(BF16) for l in range(4)]
+        others = (xb, hb, g1, g_rows)
+        part_width = width // plan.peers
+        for z in range(plan.chips):
+            for l in range(4):
+                at = slice(l * rank, (l + 1) * rank)
+                both = expand(sides[l], others[l][:, 2 * z * part_width : 2 * (z + 1) * part_width])
+                even, odd = both[:, :part_width], both[:, part_width:]
+                keep[z, at, :] = jnp.where(parity == 0, even, odd)
+                give[z, at, :] = jnp.where(parity == 0, odd, even).astype(BF16)
+
+    if first:
+        gather_terms()
+    else:
+        pl.when(any_held == 1)(gather_terms)
+
+        @pl.when(any_held == 0)
+        def _():
+            keep[...] = jnp.zeros(keep.shape, keep.dtype)
+            give[...] = jnp.zeros(give.shape, give.dtype)
 
     @pl.loop(0, capacity)
     def _(k):
@@ -454,7 +479,7 @@
             jax.ShapeDtypeStruct(part, jnp.float32),
             jax.ShapeDtypeStruct(part, BF16),
         ],
-        in_specs=[SMEM] * len(tables) + [HBM] * len(flat) + [vmem] * 3 + [HBM] * len(carried),
+        in_specs=[SMEM] * len(tables) + [HBM] * len(flat) + [HBM, vmem, vmem] + [HBM] * len(carried),
         out_specs=[HBM, vmem, vmem],
         input_output_aliases={} if first else {len(operands) - 1: 0},
         scratch_shapes=[
@@ -465,9 +490,12 @@
             pltpu.VMEM((rows, width), BF16),
             pltpu.VMEM((group * MB, width), jnp.float32),
             pltpu.VMEM((4, rows, rank), jnp.float32),
+            pltpu.VMEM((rows, width), BF16),
             pltpu.SemaphoreType.DMA((capacity,)),
             pltpu.SemaphoreType.DMA((capacity,)),
+            pltpu.SemaphoreType.DMA,
             pltpu.SMEM((capacity,), jnp.int32),
+            pltpu.SMEM((1,), jnp.int32),
         ],
         compiler_params=pltpu.CompilerParams(vmem_limit_bytes=VMEM_LIMIT),
         cost_estimate=pl.CostEstimate(
@@ -517,11 +545,10 @@
         weight[0].reshape(layers * rank // MB, MB, width) for weight in (adapter_in, adapter_out)
     ]
     spilling = plan.spill > 0
-    sent = run_send(plan, (0, 0), routes, blocks, halves, spilling)
-    w_own = lax.ppermute(sent[0], axes, hop_pairs(plan, 1, 0))
-    spilled = to_sibling(plan, sent[1]) if spilling else None
-    sent = run_send(plan, plan.sets[0], routes, blocks)
-    early = exchange(plan, sent)
+    sent = run_send(plan, plan.sets[0], routes, blocks, halves, spilling)
+    w_own = lax.ppermute(sent[chips], axes, hop_pairs(plan, 1, 0))
+    spilled = to_sibling(plan, sent[-1]) if spilling else None
+    early = exchange(plan, sent[:chips])
     tables = run_tables(plan, routes)
     sent = run_send(plan, plan.sets[1], routes, blocks, spilled=spilled)
     late = exchange(plan, sent)
@@ -534,9 +561,8 @@
     def step_more(table, sources, handed):
         return run_step(plan, rank, small_group, [table], [sources], prepared, handed)
 
-    shared = share(early)
-    handed, keep, give = run_step(plan, rank, group, tables[:1], [shared], prepared)
-    parts = [keep, to_sibling(plan, give)]
+    sources = [share(early), share(late)]
+    handed, keep, give = run_step(plan, rank, group, tables[:2], sources, prepared)
     if spilling:
 
         def direct(handed, keep):
@@ -544,11 +570,8 @@
             handed, more, gift = step_more(tables[2], share(extra), handed)
             return handed, keep + more + to_sibling(plan, gift).astype(jnp.float32)
 
-        handed, parts[0] = lax.cond(
-            tables[3][0] == 1, lambda *kept: kept, direct, handed, parts[0]
-        )
-    handed, keep, give = step_more(tables[1], share(late), handed)
-    parts += [keep, to_sibling(plan, give)]
+        handed, keep = lax.cond(tables[3][0] == 1, lambda *kept: kept, direct, handed, keep)
+    parts = [keep, to_sibling(plan, give)]
     part_width = width // peers
     vmem = pl.BlockSpec(memory_space=pltpu.VMEM)
     summed = pl.pallas_call(

time: 119 us -> 111 us (0.933)
  Pallas kernels: 29.2 us -> 21.7 us
  local copies, waits for them, and re-layouts: 4.78 us -> 6.29 us
    ppermute x1, waiting for transfers between devices: 0.01 us -> 15.4 us  [shards(): w_near = lax.ppermute(w_own, 'peer', [(p, p ^ 2) for p in range(peers)])]
    ppermute x8, waiting for transfers between devices: 35 us -> 19.9 us  [exchange(): lax.ppermute(buffers[e], ('section', 'peer'), hop_pairs(plan, 1, 2 * e))]
    pallas_call x2 -> x1, Pallas kernels: 14.8 us -> 9.56 us  [run_step(): pl.pallas_call(functools.partial(step_kernel, plan, rank, group, counts,...]
    pallas_call x3 -> x2, Pallas kernels: 9.11 us -> 6.94 us  [run_send(): pl.pallas_call(functools.partial(send_kernel, plan, span, bool(weights),...]
    ppermute x8, starting transfers between devices: 18.2 us -> 20.4 us  [exchange(): lax.ppermute(buffers[e], ('section', 'peer'), hop_pairs(plan, 1, 2 * e))]
    ppermute x13 -> x12, waiting for transfers between devices: 3.04 us -> 1 us  [to_sibling(): return lax.ppermute(array, 'peer', [(p, p ^ 1) for p in range(plan.peers)])]
    unnamed x22 -> x28, local copies, waits for them, and re-layouts: 4.11 us -> 5.62 us
    ppermute x4, starting transfers between devices: 9.18 us -> 7.7 us  [shards(): lax.ppermute(summed[e], axes, hop_pairs(plan, -1, 2 * e))]
  transfers between devices with their start and end apart: 27 -> 26, of which waited for: 11 -> 9; matrix products, arithmetic and copies ran while one was open for 0% -> 0% of each run, Pallas kernels for 19% -> 7%
where the time goes in v2:
time: 111 us
  waiting for transfers between devices  48 us (43%)
  starting transfers between devices  33.1 us (30%)
  Pallas kernels  21.7 us (20%)
  local copies, waits for them, and re-layouts  6.29 us (6%)
  between operations  1.48 us (1%)
    ppermute x8, starting transfers between devices, exchange(): lax.ppermute(buffers[e], ('section', 'peer'), hop_pairs(plan, 1, 2 * e))  20.4 us
    ppermute x8, waiting for transfers between devices, exchange(): lax.ppermute(buffers[e], ('section', 'peer'), hop_pairs(plan, 1, 2 * e))  19.9 us
    ppermute x1, waiting for transfers between devices, shards(): w_near = lax.ppermute(w_own, 'peer', [(p, p ^ 2) for p in range(peers)])  15.4 us
    pallas_call x1, Pallas kernels, run_step(): pl.pallas_call(functools.partial(step_kernel, plan, rank, group, counts,...  9.56 us
    ppermute x4, starting transfers between devices, shards(): lax.ppermute(summed[e], axes, hop_pairs(plan, -1, 2 * e))  7.7 us
    pallas_call x2, Pallas kernels, run_send(): pl.pallas_call(functools.partial(send_kernel, plan, span, bool(weights),...  6.94 us
    ppermute x4, waiting for transfers between devices, shards(): lax.ppermute(summed[e], axes, hop_pairs(plan, -1, 2 * e))  6.39 us
    unnamed x28, local copies, waits for them, and re-layouts  5.62 us
  transfers between devices with their start and end apart: 26, of which 9 were waited for; matrix products, arithmetic and copies ran while one was open for 0% of the time, Pallas kernels for 7%

profile of v2, /device:TPU:0, one launch (start us, length us, event | category | flops | bytes accessed | tf_op | source)
XLA Modules:
  0.0 110.6 jit_solution(15354109056039093090)
XLA Ops:
  0.7 4.3 %shard_map.77 = (bf16[4,8,5120]{2,1,0:T(8,128)(2,1)}, bf16[4,8,5120]{2,1,0:T(8,128)(2,1)}, bf16[4,8,5120]{2,1,0:T(8,128)(2,1)}, bf16[4,8,5120]{2,1,0:T(8,128)(2,...) custom-call(s32[4,8,8]{2,1,0:T(8,128)} %routes.5, bf16[16,8,5120]{2,1,0:T(8,128)(2,1)} %bitcast.9, ...), custom_call_target="tpu_custom_call" | custom-call | tf_op jit(solution)/shard_map/pallas_call | solution.py:154
  4.9 3.0 %collective-permute-start.9 = (bf16[2,8,5120]{2,1,0:T(8,128)(2,1)}, bf16[2,8,5120]{2,1,0:T(8,128)(2,1)S(1)}, u32[]{:S(2)}, u32[]{:S(2)}) collective-permute-start(bf16[2,8,5120]{2,1,0:T(8,128)(2,1)} %get-tuple-element.66), channel_id=1, source_target_pairs={{0,8},{1,9},{2,10},{3,11},{4,12},{5,13},{6,14},{7,15},{8,16},{9,17... | collective-permute-start | bytes 491528 | tf_op jit(solution)/shard_map/ppermute | solution.py:549
  7.9 0.0 collective-permute-start.21
  7.9 5.4 %collective-permute-done.9.refs_0_ = bf16[2,8,5120]{2,1,0:T(8,128)(2,1)S(1)} collective-permute-done((bf16[2,8,5120]{2,1,0:T(8,128)(2,1)}, bf16[2,8,5120]{2,1,0:T(8,128)(2,1)S(1)}, u32[]{:S(2)}, u32[]{:S(2)}) %collective-permute-start.9) | collective-permute-done | bytes 163872 | tf_op jit(solution)/shard_map/ppermute | solution.py:549
  13.3 0.8 collective-permute-start.13
  14.1 3.4 %collective-permute-start.14 = (bf16[4,8,5120]{2,1,0:T(8,128)(2,1)}, bf16[4,8,5120]{2,1,0:T(8,128)(2,1)S(1)}, u32[]{:S(2)}, u32[]{:S(2)}) collective-permute-start(bf16[4,8,5120]{2,1,0:T(8,128)(2,1)} %get-tuple-element.73), channel_id=1, source_target_pairs={{0,10},{1,11},{2,8},{3,9},{4,14},{5,15},{6,12},{7,13},{8,18},{9,19... | collective-permute-start | bytes 983048 | tf_op jit(solution)/shard_map/ppermute | solution.py:521
  17.5 2.6 %collective-permute-start.15 = (bf16[4,8,5120]{2,1,0:T(8,128)(2,1)}, bf16[4,8,5120]{2,1,0:T(8,128)(2,1)S(1)}, u32[]{:S(2)}, u32[]{:S(2)}) collective-permute-start(bf16[4,8,5120]{2,1,0:T(8,128)(2,1)} %get-tuple-element.74), channel_id=1, source_target_pairs={{0,12},{1,13},{2,14},{3,15},{4,8},{5,9},{6,10},{7,11},{8,20},{9,21... | collective-permute-start | bytes 983048 | tf_op jit(solution)/shard_map/ppermute | solution.py:521
  20.1 0.0 collective-permute-done.11.refs_2_
  20.1 0.7 copy-done.5
  20.8 0.4 collective-permute-start.10
  21.2 15.4 %collective-permute-done.10.refs_1_ = bf16[2,8,5120]{2,1,0:T(8,128)(2,1)S(1)} collective-permute-done((bf16[2,8,5120]{2,1,0:T(8,128)(2,1)S(1)}, bf16[2,8,5120]{2,1,0:T(8,128)(2,1)S(1)}, u32[]{:S(2)}, u32[]{:S(2)}) %collective-permute-start.10) | collective-permute-done | bytes 163872 | tf_op jit(solution)/shard_map/ppermute | solution.py:555
  36.6 3.6 %collective-permute-start.16 = (bf16[4,8,5120]{2,1,0:T(8,128)(2,1)}, bf16[4,8,5120]{2,1,0:T(8,128)(2,1)S(1)}, u32[]{:S(2)}, u32[]{:S(2)}) collective-permute-start(bf16[4,8,5120]{2,1,0:T(8,128)(2,1)} %get-tuple-element.75), channel_id=1, source_target_pairs={{0,14},{1,15},{2,12},{3,13},{4,10},{5,11},{6,8},{7,9},{8,22},{9,23... | collective-permute-start | bytes 983048 | tf_op jit(solution)/shard_map/ppermute | solution.py:521
  40.2 0.0 collective-permute-done.13.refs_2_
  40.2 0.0 collective-permute-start.17
  40.2 0.0 collective-permute-done.14.refs_3_
  40.2 0.5 collective-permute-start.18
  40.7 0.0 collective-permute-done.15.refs_4_
  40.7 0.1 collective-permute-start.19
  40.8 0.0 collective-permute-done.21.refs_0_
  40.8 0.4 collective-permute-start.12
  41.2 2.7 %shard_map.79 = (bf16[2,8,5120]{2,1,0:T(8,128)(2,1)S(1)}, bf16[2,8,5120]{2,1,0:T(8,128)(2,1)S(1)}, bf16[2,8,5120]{2,1,0:T(8,128)(2,1)S(1)}, bf16[2,8,5120]{2,1,0:T(8,128)(2,1)S(1)}) custom-call(s32[4,8,8]{2,1,0:T(8,128)S(1)} %copy-done.15, bf16[16,8,5120]{2,1,0:T(8,128)(2,1)} %bitcast.10, bf16[4,2,8,5120]{3,2,1,0:T(8,128)(2,1)S(1)} %collective-permute-done.21.refs_0_), custom_call_target="tpu_custom_call" | custom-call | tf_op jit(solution)/shard_map/pallas_call | solution.py:154
  43.9 5.6 %collective-permute-done.16.refs_5_ = bf16[4,8,5120]{2,1,0:T(8,128)(2,1)S(1)} collective-permute-done((bf16[4,8,5120]{2,1,0:T(8,128)(2,1)}, bf16[4,8,5120]{2,1,0:T(8,128)(2,1)S(1)}, u32[]{:S(2)}, u32[]{:S(2)}) %collective-permute-start.16) | collective-permute-done | bytes 327712 | tf_op jit(solution)/shard_map/ppermute | solution.py:521
  49.5 0.7 copy-done.9
  50.2 8.1 %collective-permute-start.23 = (bf16[2,8,5120]{2,1,0:T(8,128)(2,1)S(1)}, bf16[2,8,5120]{2,1,0:T(8,128)(2,1)}, u32[]{:S(2)}, u32[]{:S(2)}) collective-permute-start(bf16[2,8,5120]{2,1,0:T(8,128)(2,1)S(1)} %get-tuple-element.78), channel_id=1, source_target_pairs={{0,10},{1,11},{2,8},{3,9},{4,14},{5,15},{6,12},{7,13},{8,18},{9,19... | collective-permute-start | bytes 491528 | tf_op jit(solution)/shard_map/ppermute | solution.py:521
  58.3 0.7 copy-done.1
  59.0 1.0 collective-permute-start.24
  60.0 0.7 copy-done.3
  60.7 0.9 collective-permute-start.25
  61.6 2.3 %collective-permute-done.23.refs_11_ = bf16[2,8,5120]{2,1,0:T(8,128)(2,1)} collective-permute-done((bf16[2,8,5120]{2,1,0:T(8,128)(2,1)S(1)}, bf16[2,8,5120]{2,1,0:T(8,128)(2,1)}, u32[]{:S(2)}, u32[]{:S(2)}) %collective-permute-start.23) | collective-permute-done | bytes 163872 | tf_op jit(solution)/shard_map/ppermute | solution.py:521
  63.9 12.0 %collective-permute-done.24.refs_12_ = bf16[2,8,5120]{2,1,0:T(8,128)(2,1)} collective-permute-done((bf16[2,8,5120]{2,1,0:T(8,128)(2,1)S(1)}, bf16[2,8,5120]{2,1,0:T(8,128)(2,1)}, u32[]{:S(2)}, u32[]{:S(2)}) %collective-permute-start.24) | collective-permute-done | bytes 163872 | tf_op jit(solution)/shard_map/ppermute | solution.py:521
  75.9 0.5 collective-permute-start.29
  76.4 2.2 %shard_map.76 = (s32[32]{0:T(128)}, s32[16]{0:T(128)}, s32[16]{0:T(128)S(1)}, s32[1]{0:T(128)}) custom-call(s32[4,8,8]{2,1,0:T(8,128)S(1)} %copy-done.15), custom_call_target="tpu_custom_call" | custom-call | tf_op jit(solution)/shard_map/pallas_call | solution.py:221
  78.7 0.0 copy-start.2
  78.7 1.0 copy-done.6
  79.7 0.9 copy-done.8
  80.6 0.9 copy-done.10
  81.5 2.9 %shard_map.78 = (bf16[160,5120]{1,0:T(8,128)(2,1)}, bf16[2,2,16,5120]{3,2,1,0:T(8,128)(2,1)S(1)}, bf16[160,16]{1,0:T(8,128)(2,1)S(1)}) custom-call(bf16[20,8,5120]{2,1,0:T(8,128)(2,1)S(1)} %bitcast.8, bf16[2,8,5120]{2,1,0:T(8,128)(2,1)S(1)} %collective-permute-done.9.refs_0_, bf16[2,8,5120]{2,1,0:T(8,128)(2,1)S(1)} %copy-done.8, ...), custom_call_target="tpu_custom_call" | custom-call | tf_op jit(solution)/shard_map/pallas_call | solution.py:286
  84.5 9.6 %shard_map.80 = (bf16[20,8,5120]{2,1,0:T(8,128)(2,1)}, f32[4,64,640]{2,1,0:T(8,128)S(1)}, bf16[4,64,640]{2,1,0:T(8,128)(2,1)S(1)}) custom-call(s32[32]{0:T(128)S(1)} %copy-done.11, s32[16]{0:T(128)S(1)} %copy-done.12, bf16[4,8,5120]{2,1,0:T(8,128)(2,1)S(1)} %collective-permute-done.13.refs_2_, bf16[4,8,5120]{2,1,0:T(8,128)(2,1)S(1)} %collective-permute-done.14.refs_3_, ...), custom_call_target="tpu_custom_call" | custom-call | flops 288358400 | bytes 4915200 | tf_op jit(solution)/shard_map/pallas_call | solution.py:475
  94.0 0.1 collective-permute-start.30
  94.8 1.0 collective-permute-done.30.refs_1_
  95.7 0.1 shard_map.81
  95.8 2.4 %collective-permute-start.31 = (bf16[64,640]{1,0:T(8,128)(2,1)S(1)}, bf16[64,640]{1,0:T(8,128)(2,1)S(1)}, u32[]{:S(2)}, u32[]{:S(2)}) collective-permute-start(bf16[64,640]{1,0:T(8,128)(2,1)S(1)} %get-tuple-element.86), channel_id=1, source_target_pairs={{0,30},{1,31},{2,28},{3,29},{4,26},{5,27},{6,24},{7,25},{8,6},{9,7... | collective-permute-start | bytes 245768 | tf_op jit(solution)/shard_map/ppermute | solution.py:585
  98.2 4.0 %collective-permute-start.32 = (bf16[64,640]{1,0:T(8,128)(2,1)S(1)}, bf16[64,640]{1,0:T(8,128)(2,1)S(1)}, u32[]{:S(2)}, u32[]{:S(2)}) collective-permute-start(bf16[64,640]{1,0:T(8,128)(2,1)S(1)} %get-tuple-element.87), channel_id=1, source_target_pairs={{0,28},{1,29},{2,30},{3,31},{4,24},{5,25},{6,26},{7,27},{8,4},{9,5... | collective-permute-start | bytes 245768 | tf_op jit(solution)/shard_map/ppermute | solution.py:585
  102.2 1.3 %collective-permute-start.34 = (bf16[64,640]{1,0:T(8,128)(2,1)S(1)}, bf16[64,640]{1,0:T(8,128)(2,1)S(1)}, u32[]{:S(2)}, u32[]{:S(2)}) collective-permute-start(bf16[64,640]{1,0:T(8,128)(2,1)S(1)} %get-tuple-element.89), channel_id=1, source_target_pairs={{0,24},{1,25},{2,26},{3,27},{4,28},{5,29},{6,30},{7,31},{8,0},{9,1... | collective-permute-start | bytes 245768 | tf_op jit(solution)/shard_map/ppermute | solution.py:585
  103.5 5.6 %collective-permute-done.32 = bf16[64,640]{1,0:T(8,128)(2,1)S(1)} collective-permute-done((bf16[64,640]{1,0:T(8,128)(2,1)S(1)}, bf16[64,640]{1,0:T(8,128)(2,1)S(1)}, u32[]{:S(2)}, u32[]{:S(2)}) %collective-permute-start.32) | collective-permute-done | bytes 81952 | tf_op jit(solution)/shard_map/ppermute | solution.py:585
  109.1 0.2 collective-permute-done.33
  109.3 0.6 collective-permute-done.34
  109.9 0.7 fusion
  (41 shorter events, 0.1 us)
Async XLA Ops:
  0.6 40.6 %copy-start.15 = (s32[4,8,8]{2,1,0:T(8,128)S(1)}, s32[4,8,8]{2,1,0:T(8,128)}, u32[]{:S(2)}) copy-start(s32[4,8,8]{2,1,0:T(8,128)} %routes.5) | copy-start | bytes 3076
  0.6 78.0 %copy-start = (bf16[1,1,160,5120]{3,2,1,0:T(8,128)(2,1)S(1)}, bf16[1,1,160,5120]{3,2,1,0:T(8,128)(2,1)}, u32[]{:S(2)}) copy-start(bf16[1,1,160,5120]{3,2,1,0:T(8,128)(2,1)} %param.11) | copy-start | bytes 4915204
  4.9 8.3 %collective-permute-start.9 = (bf16[2,8,5120]{2,1,0:T(8,128)(2,1)}, bf16[2,8,5120]{2,1,0:T(8,128)(2,1)S(1)}, u32[]{:S(2)}, u32[]{:S(2)}) collective-permute-start(bf16[2,8,5120]{2,1,0:T(8,128)(2,1)} %get-tuple-element.66), channel_id=1, source_target_pairs={{0,8},{1,9},{2,10},{3,11},{4,12},{5,13},{6,14},{7,15},{8,16},{9,17... | collective-permute-start | bytes 491528 | tf_op jit(solution)/shard_map/ppermute | solution.py:549
  7.9 32.9 %collective-permute-start.21 = (bf16[4,2,8,5120]{3,2,1,0:T(8,128)(2,1)}, bf16[4,2,8,5120]{3,2,1,0:T(8,128)(2,1)S(1)}, u32[]{:S(2)}, u32[]{:S(2)}) collective-permute-start(bf16[4,2,8,5120]{3,2,1,0:T(8,128)(2,1)} %get-tuple-element.76), channel_id=1, source_target_pairs={{0,1},{1,0},{2,3},{3,2},{4,5},{5,4},{6,7},{7,6},{8,9},{9,8},{10,11... | collective-permute-start | bytes 1966088 | tf_op jit(solution)/shard_map/ppermute | solution.py:44
  13.3 6.8 %collective-permute-start.11 = (bf16[2,8,5120]{2,1,0:T(8,128)(2,1)S(1)}, bf16[2,8,5120]{2,1,0:T(8,128)(2,1)S(1)}, u32[]{:S(2)}, u32[]{:S(2)}) collective-permute-start(bf16[2,8,5120]{2,1,0:T(8,128)(2,1)S(1)} %collective-permute-done.9.refs_0_), channel_id=1, source_target_pairs={{0,1},{1,0},{2,3},{3,2},{4,5},{5,4},{6,7},{7,6},{8,9},{9,8},{10,11... | collective-permute-start | bytes 491528 | tf_op jit(solution)/shard_map/ppermute | solution.py:44
  13.3 26.9 %collective-permute-start.13 = (bf16[4,8,5120]{2,1,0:T(8,128)(2,1)}, bf16[4,8,5120]{2,1,0:T(8,128)(2,1)S(1)}, u32[]{:S(2)}, u32[]{:S(2)}) collective-permute-start(bf16[4,8,5120]{2,1,0:T(8,128)(2,1)} %get-tuple-element.72), channel_id=1, source_target_pairs={{0,8},{1,9},{2,10},{3,11},{4,12},{5,13},{6,14},{7,15},{8,16},{9,17... | collective-permute-start | bytes 983048 | tf_op jit(solution)/shard_map/ppermute | solution.py:521
  14.1 26.1 %collective-permute-start.14 = (bf16[4,8,5120]{2,1,0:T(8,128)(2,1)}, bf16[4,8,5120]{2,1,0:T(8,128)(2,1)S(1)}, u32[]{:S(2)}, u32[]{:S(2)}) collective-permute-start(bf16[4,8,5120]{2,1,0:T(8,128)(2,1)} %get-tuple-element.73), channel_id=1, source_target_pairs={{0,10},{1,11},{2,8},{3,9},{4,14},{5,15},{6,12},{7,13},{8,18},{9,19... | collective-permute-start | bytes 983048 | tf_op jit(solution)/shard_map/ppermute | solution.py:521
  17.5 23.2 %collective-permute-start.15 = (bf16[4,8,5120]{2,1,0:T(8,128)(2,1)}, bf16[4,8,5120]{2,1,0:T(8,128)(2,1)S(1)}, u32[]{:S(2)}, u32[]{:S(2)}) collective-permute-start(bf16[4,8,5120]{2,1,0:T(8,128)(2,1)} %get-tuple-element.74), channel_id=1, source_target_pairs={{0,12},{1,13},{2,14},{3,15},{4,8},{5,9},{6,10},{7,11},{8,20},{9,21... | collective-permute-start | bytes 983048 | tf_op jit(solution)/shard_map/ppermute | solution.py:521
  20.1 0.7 copy-start.5
  20.8 15.8 %collective-permute-start.10 = (bf16[2,8,5120]{2,1,0:T(8,128)(2,1)S(1)}, bf16[2,8,5120]{2,1,0:T(8,128)(2,1)S(1)}, u32[]{:S(2)}, u32[]{:S(2)}) collective-permute-start(bf16[2,8,5120]{2,1,0:T(8,128)(2,1)S(1)} %collective-permute-done.9.refs_0_), channel_id=1, source_target_pairs={{0,2},{1,3},{2,0},{3,1},{4,6},{5,7},{6,4},{7,5},{8,10},{9,11},{10,... | collective-permute-start | bytes 491528 | tf_op jit(solution)/shard_map/ppermute | solution.py:555
  36.6 23.4 %copy-start.7 = (bf16[2,8,5120]{2,1,0:T(8,128)(2,1)}, bf16[2,8,5120]{2,1,0:T(8,128)(2,1)S(1)}, u32[]{:S(2)}) copy-start(bf16[2,8,5120]{2,1,0:T(8,128)(2,1)S(1)} %collective-permute-done.10.refs_1_) | copy-start | bytes 491524
  36.6 12.9 %collective-permute-start.16 = (bf16[4,8,5120]{2,1,0:T(8,128)(2,1)}, bf16[4,8,5120]{2,1,0:T(8,128)(2,1)S(1)}, u32[]{:S(2)}, u32[]{:S(2)}) collective-permute-start(bf16[4,8,5120]{2,1,0:T(8,128)(2,1)} %get-tuple-element.75), channel_id=1, source_target_pairs={{0,14},{1,15},{2,12},{3,13},{4,10},{5,11},{6,8},{7,9},{8,22},{9,23... | collective-permute-start | bytes 983048 | tf_op jit(solution)/shard_map/ppermute | solution.py:521
  40.2 10.0 %collective-permute-start.17 = (bf16[4,8,5120]{2,1,0:T(8,128)(2,1)S(1)}, bf16[4,8,5120]{2,1,0:T(8,128)(2,1)S(1)}, u32[]{:S(2)}, u32[]{:S(2)}) collective-permute-start(bf16[4,8,5120]{2,1,0:T(8,128)(2,1)S(1)} %collective-permute-done.13.refs_2_), channel_id=1, source_target_pairs={{0,1},{1,0},{2,3},{3,2},{4,5},{5,4},{6,7},{7,6},{8,9},{9,8},{10,11... | collective-permute-start | bytes 983048 | tf_op jit(solution)/shard_map/ppermute | solution.py:44
  40.2 18.1 %collective-permute-start.18 = (bf16[4,8,5120]{2,1,0:T(8,128)(2,1)S(1)}, bf16[4,8,5120]{2,1,0:T(8,128)(2,1)S(1)}, u32[]{:S(2)}, u32[]{:S(2)}) collective-permute-start(bf16[4,8,5120]{2,1,0:T(8,128)(2,1)S(1)} %collective-permute-done.14.refs_3_), channel_id=1, source_target_pairs={{0,1},{1,0},{2,3},{3,2},{4,5},{5,4},{6,7},{7,6},{8,9},{9,8},{10,11... | collective-permute-start | bytes 983048 | tf_op jit(solution)/shard_map/ppermute | solution.py:44
  40.7 19.3 %collective-permute-start.19 = (bf16[4,8,5120]{2,1,0:T(8,128)(2,1)S(1)}, bf16[4,8,5120]{2,1,0:T(8,128)(2,1)S(1)}, u32[]{:S(2)}, u32[]{:S(2)}) collective-permute-start(bf16[4,8,5120]{2,1,0:T(8,128)(2,1)S(1)} %collective-permute-done.15.refs_4_), channel_id=1, source_target_pairs={{0,1},{1,0},{2,3},{3,2},{4,5},{5,4},{6,7},{7,6},{8,9},{9,8},{10,11... | collective-permute-start | bytes 983048 | tf_op jit(solution)/shard_map/ppermute | solution.py:44
  40.8 8.7 %collective-permute-start.12 = (bf16[2,8,5120]{2,1,0:T(8,128)(2,1)S(1)}, bf16[2,8,5120]{2,1,0:T(8,128)(2,1)S(1)}, u32[]{:S(2)}, u32[]{:S(2)}) collective-permute-start(bf16[2,8,5120]{2,1,0:T(8,128)(2,1)S(1)} %collective-permute-done.10.refs_1_), channel_id=1, source_target_pairs={{0,1},{1,0},{2,3},{3,2},{4,5},{5,4},{6,7},{7,6},{8,9},{9,8},{10,11... | collective-permute-start | bytes 491528 | tf_op jit(solution)/shard_map/ppermute | solution.py:44
  49.5 34.9 %collective-permute-start.20 = (bf16[4,8,5120]{2,1,0:T(8,128)(2,1)S(1)}, bf16[4,8,5120]{2,1,0:T(8,128)(2,1)}, u32[]{:S(2)}, u32[]{:S(2)}) collective-permute-start(bf16[4,8,5120]{2,1,0:T(8,128)(2,1)S(1)} %collective-permute-done.16.refs_5_), channel_id=1, source_target_pairs={{0,1},{1,0},{2,3},{3,2},{4,5},{5,4},{6,7},{7,6},{8,9},{9,8},{10,11... | collective-permute-start | bytes 983048 | tf_op jit(solution)/shard_map/ppermute | solution.py:44
  49.5 0.7 copy-start.9
  50.2 11.5 %collective-permute-start.22 = (bf16[2,8,5120]{2,1,0:T(8,128)(2,1)S(1)}, bf16[2,8,5120]{2,1,0:T(8,128)(2,1)}, u32[]{:S(2)}, u32[]{:S(2)}) collective-permute-start(bf16[2,8,5120]{2,1,0:T(8,128)(2,1)S(1)} %get-tuple-element.77), channel_id=1, source_target_pairs={{0,8},{1,9},{2,10},{3,11},{4,12},{5,13},{6,14},{7,15},{8,16},{9,17... | collective-permute-start | bytes 491528 | tf_op jit(solution)/shard_map/ppermute | solution.py:521
  50.2 13.7 %collective-permute-start.23 = (bf16[2,8,5120]{2,1,0:T(8,128)(2,1)S(1)}, bf16[2,8,5120]{2,1,0:T(8,128)(2,1)}, u32[]{:S(2)}, u32[]{:S(2)}) collective-permute-start(bf16[2,8,5120]{2,1,0:T(8,128)(2,1)S(1)} %get-tuple-element.78), channel_id=1, source_target_pairs={{0,10},{1,11},{2,8},{3,9},{4,14},{5,15},{6,12},{7,13},{8,18},{9,19... | collective-permute-start | bytes 491528 | tf_op jit(solution)/shard_map/ppermute | solution.py:521
  58.3 0.7 copy-start.1
  59.0 16.9 %collective-permute-start.24 = (bf16[2,8,5120]{2,1,0:T(8,128)(2,1)S(1)}, bf16[2,8,5120]{2,1,0:T(8,128)(2,1)}, u32[]{:S(2)}, u32[]{:S(2)}) collective-permute-start(bf16[2,8,5120]{2,1,0:T(8,128)(2,1)S(1)} %get-tuple-element.79), channel_id=1, source_target_pairs={{0,12},{1,13},{2,14},{3,15},{4,8},{5,9},{6,10},{7,11},{8,20},{9,21... | collective-permute-start | bytes 491528 | tf_op jit(solution)/shard_map/ppermute | solution.py:521
  60.0 0.7 copy-start.3
  60.7 15.2 %collective-permute-start.25 = (bf16[2,8,5120]{2,1,0:T(8,128)(2,1)S(1)}, bf16[2,8,5120]{2,1,0:T(8,128)(2,1)}, u32[]{:S(2)}, u32[]{:S(2)}) collective-permute-start(bf16[2,8,5120]{2,1,0:T(8,128)(2,1)S(1)} %get-tuple-element.80), channel_id=1, source_target_pairs={{0,14},{1,15},{2,12},{3,13},{4,10},{5,11},{6,8},{7,9},{8,22},{9,23... | collective-permute-start | bytes 491528 | tf_op jit(solution)/shard_map/ppermute | solution.py:521
  61.6 22.7 %collective-permute-start.26 = (bf16[2,8,5120]{2,1,0:T(8,128)(2,1)}, bf16[2,8,5120]{2,1,0:T(8,128)(2,1)}, u32[]{:S(2)}, u32[]{:S(2)}) collective-permute-start(bf16[2,8,5120]{2,1,0:T(8,128)(2,1)} %collective-permute-done.22.refs_10_), channel_id=1, source_target_pairs={{0,1},{1,0},{2,3},{3,2},{4,5},{5,4},{6,7},{7,6},{8,9},{9,8},{10,11... | collective-permute-start | bytes 491528 | tf_op jit(solution)/shard_map/ppermute | solution.py:44
  63.9 20.5 %collective-permute-start.27 = (bf16[2,8,5120]{2,1,0:T(8,128)(2,1)}, bf16[2,8,5120]{2,1,0:T(8,128)(2,1)}, u32[]{:S(2)}, u32[]{:S(2)}) collective-permute-start(bf16[2,8,5120]{2,1,0:T(8,128)(2,1)} %collective-permute-done.23.refs_11_), channel_id=1, source_target_pairs={{0,1},{1,0},{2,3},{3,2},{4,5},{5,4},{6,7},{7,6},{8,9},{9,8},{10,11... | collective-permute-start | bytes 491528 | tf_op jit(solution)/shard_map/ppermute | solution.py:44
  75.9 8.5 %collective-permute-start.28 = (bf16[2,8,5120]{2,1,0:T(8,128)(2,1)}, bf16[2,8,5120]{2,1,0:T(8,128)(2,1)}, u32[]{:S(2)}, u32[]{:S(2)}) collective-permute-start(bf16[2,8,5120]{2,1,0:T(8,128)(2,1)} %collective-permute-done.24.refs_12_), channel_id=1, source_target_pairs={{0,1},{1,0},{2,3},{3,2},{4,5},{5,4},{6,7},{7,6},{8,9},{9,8},{10,11... | collective-permute-start | bytes 491528 | tf_op jit(solution)/shard_map/ppermute | solution.py:44
  75.9 8.5 %collective-permute-start.29 = (bf16[2,8,5120]{2,1,0:T(8,128)(2,1)}, bf16[2,8,5120]{2,1,0:T(8,128)(2,1)}, u32[]{:S(2)}, u32[]{:S(2)}) collective-permute-start(bf16[2,8,5120]{2,1,0:T(8,128)(2,1)} %collective-permute-done.25.refs_13_), channel_id=1, source_target_pairs={{0,1},{1,0},{2,3},{3,2},{4,5},{5,4},{6,7},{7,6},{8,9},{9,8},{10,11... | collective-permute-start | bytes 491528 | tf_op jit(solution)/shard_map/ppermute | solution.py:44
  78.7 5.8 %copy-start.2 = (bf16[4,8,5120]{2,1,0:T(8,128)(2,1)S(1)}, bf16[4,8,5120]{2,1,0:T(8,128)(2,1)}, u32[]{:S(2)}) copy-start(bf16[4,8,5120]{2,1,0:T(8,128)(2,1)} %copy-done.1) | copy-start | bytes 983044
  78.7 5.8 %copy-start.4 = (bf16[4,8,5120]{2,1,0:T(8,128)(2,1)S(1)}, bf16[4,8,5120]{2,1,0:T(8,128)(2,1)}, u32[]{:S(2)}) copy-start(bf16[4,8,5120]{2,1,0:T(8,128)(2,1)} %copy-done.3) | copy-start | bytes 983044
  78.7 1.0 copy-start.6
  79.7 0.9 copy-start.8
  80.6 0.9 copy-start.10
  81.5 3.0 %copy-start.11 = (s32[32]{0:T(128)S(1)}, s32[32]{0:T(128)}, u32[]{:S(2)}) copy-start(s32[32]{0:T(128)} %get-tuple-element.70.refs_0_) | copy-start | bytes 388
  81.5 3.0 %copy-start.12 = (s32[16]{0:T(128)S(1)}, s32[16]{0:T(128)}, u32[]{:S(2)}) copy-start(s32[16]{0:T(128)} %get-tuple-element.71.refs_1_) | copy-start | bytes 196
  94.0 1.7 %collective-permute-start.30 = (bf16[4,64,640]{2,1,0:T(8,128)(2,1)S(1)}, bf16[4,64,640]{2,1,0:T(8,128)(2,1)S(1)}, u32[]{:S(2)}, u32[]{:S(2)}) collective-permute-start(bf16[4,64,640]{2,1,0:T(8,128)(2,1)S(1)} %get-tuple-element.85), channel_id=1, source_target_pairs={{0,1},{1,0},{2,3},{3,2},{4,5},{5,4},{6,7},{7,6},{8,9},{9,8},{10,11... | collective-permute-start | bytes 983048 | tf_op jit(solution)/shard_map/ppermute | solution.py:44
  95.8 7.7 %collective-permute-start.31 = (bf16[64,640]{1,0:T(8,128)(2,1)S(1)}, bf16[64,640]{1,0:T(8,128)(2,1)S(1)}, u32[]{:S(2)}, u32[]{:S(2)}) collective-permute-start(bf16[64,640]{1,0:T(8,128)(2,1)S(1)} %get-tuple-element.86), channel_id=1, source_target_pairs={{0,30},{1,31},{2,28},{3,29},{4,26},{5,27},{6,24},{7,25},{8,6},{9,7... | collective-permute-start | bytes 245768 | tf_op jit(solution)/shard_map/ppermute | solution.py:585
  98.2 10.9 %collective-permute-start.32 = (bf16[64,640]{1,0:T(8,128)(2,1)S(1)}, bf16[64,640]{1,0:T(8,128)(2,1)S(1)}, u32[]{:S(2)}, u32[]{:S(2)}) collective-permute-start(bf16[64,640]{1,0:T(8,128)(2,1)S(1)} %get-tuple-element.87), channel_id=1, source_target_pairs={{0,28},{1,29},{2,30},{3,31},{4,24},{5,25},{6,26},{7,27},{8,4},{9,5... | collective-permute-start | bytes 245768 | tf_op jit(solution)/shard_map/ppermute | solution.py:585
  102.2 7.1 %collective-permute-start.33 = (bf16[64,640]{1,0:T(8,128)(2,1)S(1)}, bf16[64,640]{1,0:T(8,128)(2,1)S(1)}, u32[]{:S(2)}, u32[]{:S(2)}) collective-permute-start(bf16[64,640]{1,0:T(8,128)(2,1)S(1)} %get-tuple-element.88), channel_id=1, source_target_pairs={{0,26},{1,27},{2,24},{3,25},{4,30},{5,31},{6,28},{7,29},{8,2},{9,3... | collective-permute-start | bytes 245768 | tf_op jit(solution)/shard_map/ppermute | solution.py:585
  102.2 7.7 %collective-permute-start.34 = (bf16[64,640]{1,0:T(8,128)(2,1)S(1)}, bf16[64,640]{1,0:T(8,128)(2,1)S(1)}, u32[]{:S(2)}, u32[]{:S(2)}) collective-permute-start(bf16[64,640]{1,0:T(8,128)(2,1)S(1)} %get-tuple-element.89), channel_id=1, source_target_pairs={{0,24},{1,25},{2,26},{3,27},{4,28},{5,29},{6,30},{7,31},{8,0},{9,1... | collective-permute-start | bytes 245768 | tf_op jit(solution)/shard_map/ppermute | solution.py:585

commit v3 on v2

--- a/solution.py
+++ b/solution.py
@@ -10,7 +10,7 @@
 
 MB = 8
 EPSILON = 1e-06
-VMEM_LIMIT = 20 * 2**20
+VMEM_LIMIT = 16 * 2**20
 SEND_LIMIT = 8 * 2**20
 PREPARE_LIMIT = 12 * 2**20
 
@@ -27,7 +27,8 @@
         mean = max(1, 2 * micro // peers)
         self.full = 2 * mean
         self.sent = min(self.full, mean + (mean + 1) // 2)
-        self.sets = [(0, mean), (mean, self.sent)]
+        first = max(1, 3 * mean // 4)
+        self.sets = [(0, first), (first, self.sent)]
         self.extra = (self.sent, self.full)
         self.spill = min(self.full - self.sent, self.sent - mean)
 
@@ -545,10 +546,13 @@
         weight[0].reshape(layers * rank // MB, MB, width) for weight in (adapter_in, adapter_out)
     ]
     spilling = plan.spill > 0
-    sent = run_send(plan, plan.sets[0], routes, blocks, halves, spilling)
+    sent = run_send(plan, plan.sets[0], routes, blocks, halves)
     w_own = lax.ppermute(sent[chips], axes, hop_pairs(plan, 1, 0))
-    spilled = to_sibling(plan, sent[-1]) if spilling else None
     early = exchange(plan, sent[:chips])
+    spilled = None
+    if spilling:
+        spilled = run_send(plan, (0, 0), routes, blocks, spilling=True)[0]
+        spilled = to_sibling(plan, spilled)
     tables = run_tables(plan, routes)
     sent = run_send(plan, plan.sets[1], routes, blocks, spilled=spilled)
     late = exchange(plan, sent)

time: 111 us -> 112 us (level)
  Pallas kernels: 21.7 us -> 24.5 us
  waiting for transfers between devices: 48 us -> 46.3 us
    ppermute x1, waiting for transfers between devices: 15.4 us -> 1.28 us  [shards(): w_near = lax.ppermute(w_own, 'peer', [(p, p ^ 2) for p in range(peers)])]
    ppermute x1, waiting for transfers between devices: 5.39 us -> 15.3 us  [shards(): w_own = lax.ppermute(sent[chips], axes, hop_pairs(plan, 1, 0))]
    pallas_call x2 -> x3, Pallas kernels: 6.94 us -> 9.66 us  [run_send(): pl.pallas_call(functools.partial(send_kernel, plan, span, bool(weights),...]
    ppermute x8, waiting for transfers between devices: 19.9 us -> 22.5 us  [exchange(): lax.ppermute(buffers[e], ('section', 'peer'), hop_pairs(plan, 1, 2 * e))]
    ppermute x8, starting transfers between devices: 20.4 us -> 17.9 us  [exchange(): lax.ppermute(buffers[e], ('section', 'peer'), hop_pairs(plan, 1, 2 * e))]
    ppermute x1, starting transfers between devices: 2.96 us -> 1.49 us  [shards(): w_own = lax.ppermute(sent[chips], axes, hop_pairs(plan, 1, 0))]
    ppermute x1, starting transfers between devices: 0.45 us -> 1.77 us  [shards(): w_near = lax.ppermute(w_own, 'peer', [(p, p ^ 2) for p in range(peers)])]
  transfers between devices with their start and end apart: 26 -> 26, of which waited for: 9 -> 9; matrix products, arithmetic and copies ran while one was open for 0% -> 0% of each run, Pallas kernels for 7% -> 10%
where the time goes in v3:
time: 112 us; the launch traced here: 111 us
  waiting for transfers between devices  46.3 us (41%)
  starting transfers between devices  32.6 us (29%)
  Pallas kernels  24.5 us (22%)
  local copies, waits for them, and re-layouts  6.38 us (6%)
  between operations  1.39 us (1%)
    ppermute x8, waiting for transfers between devices, exchange(): lax.ppermute(buffers[e], ('section', 'peer'), hop_pairs(plan, 1, 2 * e))  22.5 us
    ppermute x8, starting transfers between devices, exchange(): lax.ppermute(buffers[e], ('section', 'peer'), hop_pairs(plan, 1, 2 * e))  17.9 us
    ppermute x1, waiting for transfers between devices, shards(): w_own = lax.ppermute(sent[chips], axes, hop_pairs(plan, 1, 0))  15.3 us
    pallas_call x1, Pallas kernels, run_step(): pl.pallas_call(functools.partial(step_kernel, plan, rank, group, counts,...  9.73 us
    pallas_call x3, Pallas kernels, run_send(): pl.pallas_call(functools.partial(send_kernel, plan, span, bool(weights),...  9.66 us
    ppermute x4, starting transfers between devices, shards(): lax.ppermute(summed[e], axes, hop_pairs(plan, -1, 2 * e))  8.76 us
    ppermute x4, waiting for transfers between devices, shards(): lax.ppermute(summed[e], axes, hop_pairs(plan, -1, 2 * e))  6.13 us
    unnamed x28, local copies, waits for them, and re-layouts  5.7 us
  transfers between devices with their start and end apart: 26, of which 9 were waited for; matrix products, arithmetic and copies ran while one was open for 0% of the time, Pallas kernels for 10%

profile of v3, /device:TPU:0, one launch (start us, length us, event | category | flops | bytes accessed | tf_op | source)
XLA Modules:
  0.0 111.3 jit_solution(7213996259704864180)
XLA Ops:
  0.6 3.2 %shard_map.79 = bf16[4,2,8,5120]{3,2,1,0:T(8,128)(2,1)} custom-call(s32[4,8,8]{2,1,0:T(8,128)} %routes.7, bf16[16,8,5120]{2,1,0:T(8,128)(2,1)} %bitcast.9), custom_call_target="tpu_custom_call" | custom-call | tf_op jit(solution)/shard_map/pallas_call | solution.py:155
  3.9 0.6 collective-permute-start.21
  4.5 3.3 %shard_map.77 = (bf16[3,8,5120]{2,1,0:T(8,128)(2,1)}, bf16[3,8,5120]{2,1,0:T(8,128)(2,1)}, bf16[3,8,5120]{2,1,0:T(8,128)(2,1)}, bf16[3,8,5120]{2,1,0:T(8,128)(2,1)}, bf16[2,8,5120]{2,1,0:T(8,128)(2,1)}) custom-call(s32[4,8,8]{2,1,0:T(8,128)S(1)} %copy-done.15, bf16[16,8,5120]{2,1,0:T(8,128)(2,1)} %bitcast.10, bf16[4,8,5120]{2,1,0:T(8,128)(2,1)} %bitcast.14, ...), custom_call_target="tpu_custom_call" | custom-call | tf_op jit(solution)/shard_map/pallas_call | solution.py:155
  7.8 2.6 %collective-permute-start.13 = (bf16[3,8,5120]{2,1,0:T(8,128)(2,1)}, bf16[3,8,5120]{2,1,0:T(8,128)(2,1)S(1)}, u32[]{:S(2)}, u32[]{:S(2)}) collective-permute-start(bf16[3,8,5120]{2,1,0:T(8,128)(2,1)} %get-tuple-element.71), channel_id=1, source_target_pairs={{0,8},{1,9},{2,10},{3,11},{4,12},{5,13},{6,14},{7,15},{8,16},{9,17... | collective-permute-start | bytes 737288 | tf_op jit(solution)/shard_map/ppermute | solution.py:522
  10.3 1.5 %collective-permute-start.9 = (bf16[2,8,5120]{2,1,0:T(8,128)(2,1)}, bf16[2,8,5120]{2,1,0:T(8,128)(2,1)S(1)}, u32[]{:S(2)}, u32[]{:S(2)}) collective-permute-start(bf16[2,8,5120]{2,1,0:T(8,128)(2,1)} %get-tuple-element.65), channel_id=1, source_target_pairs={{0,8},{1,9},{2,10},{3,11},{4,12},{5,13},{6,14},{7,15},{8,16},{9,17... | collective-permute-start | bytes 491528 | tf_op jit(solution)/shard_map/ppermute | solution.py:550
  11.8 2.5 %collective-permute-start.14 = (bf16[3,8,5120]{2,1,0:T(8,128)(2,1)}, bf16[3,8,5120]{2,1,0:T(8,128)(2,1)S(1)}, u32[]{:S(2)}, u32[]{:S(2)}) collective-permute-start(bf16[3,8,5120]{2,1,0:T(8,128)(2,1)} %get-tuple-element.72), channel_id=1, source_target_pairs={{0,10},{1,11},{2,8},{3,9},{4,14},{5,15},{6,12},{7,13},{8,18},{9,19... | collective-permute-start | bytes 737288 | tf_op jit(solution)/shard_map/ppermute | solution.py:522
  14.3 2.5 %collective-permute-start.15 = (bf16[3,8,5120]{2,1,0:T(8,128)(2,1)}, bf16[3,8,5120]{2,1,0:T(8,128)(2,1)S(1)}, u32[]{:S(2)}, u32[]{:S(2)}) collective-permute-start(bf16[3,8,5120]{2,1,0:T(8,128)(2,1)} %get-tuple-element.73), channel_id=1, source_target_pairs={{0,12},{1,13},{2,14},{3,15},{4,8},{5,9},{6,10},{7,11},{8,20},{9,21... | collective-permute-start | bytes 737288 | tf_op jit(solution)/shard_map/ppermute | solution.py:522
  16.8 15.3 %collective-permute-done.9.refs_0_ = bf16[2,8,5120]{2,1,0:T(8,128)(2,1)S(1)} collective-permute-done((bf16[2,8,5120]{2,1,0:T(8,128)(2,1)}, bf16[2,8,5120]{2,1,0:T(8,128)(2,1)S(1)}, u32[]{:S(2)}, u32[]{:S(2)}) %collective-permute-start.9) | collective-permute-done | bytes 163872 | tf_op jit(solution)/shard_map/ppermute | solution.py:550
  32.1 1.8 %collective-permute-start.10 = (bf16[2,8,5120]{2,1,0:T(8,128)(2,1)S(1)}, bf16[2,8,5120]{2,1,0:T(8,128)(2,1)S(1)}, u32[]{:S(2)}, u32[]{:S(2)}) collective-permute-start(bf16[2,8,5120]{2,1,0:T(8,128)(2,1)S(1)} %collective-permute-done.9.refs_0_), channel_id=1, source_target_pairs={{0,2},{1,3},{2,0},{3,1},{4,6},{5,7},{6,4},{7,5},{8,10},{9,11},{10,... | collective-permute-start | bytes 491528 | tf_op jit(solution)/shard_map/ppermute | solution.py:559
  33.9 0.0 collective-permute-done.13.refs_2_
  33.9 2.5 %collective-permute-start.16 = (bf16[3,8,5120]{2,1,0:T(8,128)(2,1)}, bf16[3,8,5120]{2,1,0:T(8,128)(2,1)S(1)}, u32[]{:S(2)}, u32[]{:S(2)}) collective-permute-start(bf16[3,8,5120]{2,1,0:T(8,128)(2,1)} %get-tuple-element.74), channel_id=1, source_target_pairs={{0,14},{1,15},{2,12},{3,13},{4,10},{5,11},{6,8},{7,9},{8,22},{9,23... | collective-permute-start | bytes 737288 | tf_op jit(solution)/shard_map/ppermute | solution.py:522
  36.4 0.0 collective-permute-done.14.refs_3_
  36.4 0.5 collective-permute-start.18
  36.9 1.3 %collective-permute-done.10.refs_1_ = bf16[2,8,5120]{2,1,0:T(8,128)(2,1)S(1)} collective-permute-done((bf16[2,8,5120]{2,1,0:T(8,128)(2,1)S(1)}, bf16[2,8,5120]{2,1,0:T(8,128)(2,1)S(1)}, u32[]{:S(2)}, u32[]{:S(2)}) %collective-permute-start.10) | collective-permute-done | bytes 163872 | tf_op jit(solution)/shard_map/ppermute | solution.py:559
  38.2 0.0 collective-permute-start.11
  38.2 0.0 collective-permute-done.21.refs_0_
  38.2 0.5 collective-permute-start.12
  38.7 3.1 %shard_map.80 = (bf16[3,8,5120]{2,1,0:T(8,128)(2,1)S(1)}, bf16[3,8,5120]{2,1,0:T(8,128)(2,1)S(1)}, bf16[3,8,5120]{2,1,0:T(8,128)(2,1)S(1)}, bf16[3,8,5120]{2,1,0:T(8,128)(2,1)S(1)}) custom-call(s32[4,8,8]{2,1,0:T(8,128)S(1)} %copy-done.15, bf16[16,8,5120]{2,1,0:T(8,128)(2,1)} %bitcast.11, bf16[4,2,8,5120]{3,2,1,0:T(8,128)(2,1)S(1)} %collective-permute-done.21.refs_0_), custom_call_target="tpu_custom_call" | custom-call | tf_op jit(solution)/shard_map/pallas_call | solution.py:155
  41.8 4.6 %collective-permute-done.16.refs_5_ = bf16[3,8,5120]{2,1,0:T(8,128)(2,1)S(1)} collective-permute-done((bf16[3,8,5120]{2,1,0:T(8,128)(2,1)}, bf16[3,8,5120]{2,1,0:T(8,128)(2,1)S(1)}, u32[]{:S(2)}, u32[]{:S(2)}) %collective-permute-start.16) | collective-permute-done | bytes 245792 | tf_op jit(solution)/shard_map/ppermute | solution.py:522
  46.4 0.7 copy-done.7
  47.1 0.5 collective-permute-start.22
  47.6 0.7 copy-done.9
  48.3 4.3 %collective-permute-start.23 = (bf16[3,8,5120]{2,1,0:T(8,128)(2,1)S(1)}, bf16[3,8,5120]{2,1,0:T(8,128)(2,1)}, u32[]{:S(2)}, u32[]{:S(2)}) collective-permute-start(bf16[3,8,5120]{2,1,0:T(8,128)(2,1)S(1)} %get-tuple-element.76), channel_id=1, source_target_pairs={{0,10},{1,11},{2,8},{3,9},{4,14},{5,15},{6,12},{7,13},{8,18},{9,19... | collective-permute-start | bytes 737288 | tf_op jit(solution)/shard_map/ppermute | solution.py:522
  52.6 2.5 %collective-permute-start.24 = (bf16[3,8,5120]{2,1,0:T(8,128)(2,1)S(1)}, bf16[3,8,5120]{2,1,0:T(8,128)(2,1)}, u32[]{:S(2)}, u32[]{:S(2)}) collective-permute-start(bf16[3,8,5120]{2,1,0:T(8,128)(2,1)S(1)} %get-tuple-element.77), channel_id=1, source_target_pairs={{0,12},{1,13},{2,14},{3,15},{4,8},{5,9},{6,10},{7,11},{8,20},{9,21... | collective-permute-start | bytes 737288 | tf_op jit(solution)/shard_map/ppermute | solution.py:522
  55.2 0.7 copy-done.1
  55.8 0.5 collective-permute-start.25
  56.4 9.6 %collective-permute-done.22.refs_10_ = bf16[3,8,5120]{2,1,0:T(8,128)(2,1)} collective-permute-done((bf16[3,8,5120]{2,1,0:T(8,128)(2,1)S(1)}, bf16[3,8,5120]{2,1,0:T(8,128)(2,1)}, u32[]{:S(2)}, u32[]{:S(2)}) %collective-permute-start.22) | collective-permute-done | bytes 245792 | tf_op jit(solution)/shard_map/ppermute | solution.py:522
  65.9 0.5 collective-permute-start.27
  66.4 8.3 %collective-permute-done.24.refs_12_ = bf16[3,8,5120]{2,1,0:T(8,128)(2,1)} collective-permute-done((bf16[3,8,5120]{2,1,0:T(8,128)(2,1)S(1)}, bf16[3,8,5120]{2,1,0:T(8,128)(2,1)}, u32[]{:S(2)}, u32[]{:S(2)}) %collective-permute-start.24) | collective-permute-done | bytes 245792 | tf_op jit(solution)/shard_map/ppermute | solution.py:522
  74.8 0.5 collective-permute-start.29
  75.3 2.2 %shard_map.76 = (s32[24]{0:T(128)}, s32[24]{0:T(128)}, s32[16]{0:T(128)S(1)}, s32[1]{0:T(128)}) custom-call(s32[4,8,8]{2,1,0:T(8,128)S(1)} %copy-done.15), custom_call_target="tpu_custom_call" | custom-call | tf_op jit(solution)/shard_map/pallas_call | solution.py:222
  77.5 0.9 copy-done.4
  78.4 0.9 copy-done.6
  79.3 0.9 copy-done.8
  80.3 0.9 copy-done.10
  81.2 2.9 %shard_map.78 = (bf16[160,5120]{1,0:T(8,128)(2,1)}, bf16[2,2,16,5120]{3,2,1,0:T(8,128)(2,1)S(1)}, bf16[160,16]{1,0:T(8,128)(2,1)}) custom-call(bf16[20,8,5120]{2,1,0:T(8,128)(2,1)S(1)} %bitcast.8, bf16[2,8,5120]{2,1,0:T(8,128)(2,1)S(1)} %copy-done.4, bf16[2,8,5120]{2,1,0:T(8,128)(2,1)S(1)} %copy-done.6, bf16[2,8,5120]{2,1,0:T(8,128)(2,1)S(1)} %copy-done.8, ...), custom_call_target="tpu_custom_call" | custom-call | tf_op jit(solution)/shard_map/pallas_call | solution.py:287
  84.1 9.7 %shard_map.81 = (bf16[20,8,5120]{2,1,0:T(8,128)(2,1)}, f32[4,64,640]{2,1,0:T(8,128)S(1)}, bf16[4,64,640]{2,1,0:T(8,128)(2,1)S(1)}) custom-call(s32[24]{0:T(128)S(1)} %copy-done.11, s32[24]{0:T(128)S(1)} %copy-done.12, bf16[3,8,5120]{2,1,0:T(8,128)(2,1)S(1)} %collective-permute-done.13.refs_2_, bf16[3,8,5120]{2,1,0:T(8,128)(2,1)S(1)} %collective-permute-done.14.refs_3_, ...), custom_call_target="tpu_custom_call" | custom-call | flops 288358400 | bytes 4915200 | tf_op jit(solution)/shard_map/pallas_call | solution.py:476
  93.9 0.1 collective-permute-start.30
  94.5 1.0 collective-permute-done.30.refs_1_
  95.6 0.1 shard_map.82
  95.6 2.6 %collective-permute-start.31 = (bf16[64,640]{1,0:T(8,128)(2,1)S(1)}, bf16[64,640]{1,0:T(8,128)(2,1)S(1)}, u32[]{:S(2)}, u32[]{:S(2)}) collective-permute-start(bf16[64,640]{1,0:T(8,128)(2,1)S(1)} %get-tuple-element.84), channel_id=1, source_target_pairs={{0,30},{1,31},{2,28},{3,29},{4,26},{5,27},{6,24},{7,25},{8,6},{9,7... | collective-permute-start | bytes 245768 | tf_op jit(solution)/shard_map/ppermute | solution.py:589
  98.3 4.5 %collective-permute-start.32 = (bf16[64,640]{1,0:T(8,128)(2,1)S(1)}, bf16[64,640]{1,0:T(8,128)(2,1)S(1)}, u32[]{:S(2)}, u32[]{:S(2)}) collective-permute-start(bf16[64,640]{1,0:T(8,128)(2,1)S(1)} %get-tuple-element.85), channel_id=1, source_target_pairs={{0,28},{1,29},{2,30},{3,31},{4,24},{5,25},{6,26},{7,27},{8,4},{9,5... | collective-permute-start | bytes 245768 | tf_op jit(solution)/shard_map/ppermute | solution.py:589
  102.8 1.3 %collective-permute-start.33 = (bf16[64,640]{1,0:T(8,128)(2,1)S(1)}, bf16[64,640]{1,0:T(8,128)(2,1)S(1)}, u32[]{:S(2)}, u32[]{:S(2)}) collective-permute-start(bf16[64,640]{1,0:T(8,128)(2,1)S(1)} %get-tuple-element.86), channel_id=1, source_target_pairs={{0,26},{1,27},{2,24},{3,25},{4,30},{5,31},{6,28},{7,29},{8,2},{9,3... | collective-permute-start | bytes 245768 | tf_op jit(solution)/shard_map/ppermute | solution.py:589
  104.1 0.3 collective-permute-start.34
  104.4 4.4 %collective-permute-done.32 = bf16[64,640]{1,0:T(8,128)(2,1)S(1)} collective-permute-done((bf16[64,640]{1,0:T(8,128)(2,1)S(1)}, bf16[64,640]{1,0:T(8,128)(2,1)S(1)}, u32[]{:S(2)}, u32[]{:S(2)}) %collective-permute-start.32) | collective-permute-done | bytes 81952 | tf_op jit(solution)/shard_map/ppermute | solution.py:589
  108.8 0.2 collective-permute-done.33
  109.0 1.5 %collective-permute-done.34 = bf16[64,640]{1,0:T(8,128)(2,1)S(1)} collective-permute-done((bf16[64,640]{1,0:T(8,128)(2,1)S(1)}, bf16[64,640]{1,0:T(8,128)(2,1)S(1)}, u32[]{:S(2)}, u32[]{:S(2)}) %collective-permute-start.34) | collective-permute-done | bytes 81952 | tf_op jit(solution)/shard_map/ppermute | solution.py:589
  110.6 0.7 fusion
  (42 shorter events, 0.1 us)
Async XLA Ops:
  0.6 3.8 %copy-start.15 = (s32[4,8,8]{2,1,0:T(8,128)S(1)}, s32[4,8,8]{2,1,0:T(8,128)}, u32[]{:S(2)}) copy-start(s32[4,8,8]{2,1,0:T(8,128)} %routes.7) | copy-start | bytes 3076
  3.9 34.3 %collective-permute-start.21 = (bf16[4,2,8,5120]{3,2,1,0:T(8,128)(2,1)}, bf16[4,2,8,5120]{3,2,1,0:T(8,128)(2,1)S(1)}, u32[]{:S(2)}, u32[]{:S(2)}) collective-permute-start(bf16[4,2,8,5120]{3,2,1,0:T(8,128)(2,1)} %shard_map.79), channel_id=1, source_target_pairs={{0,1},{1,0},{2,3},{3,2},{4,5},{5,4},{6,7},{7,6},{8,9},{9,8},{10,11... | collective-permute-start | bytes 1966088 | tf_op jit(solution)/shard_map/ppermute | solution.py:45
  4.4 73.1 %copy-start = (bf16[1,1,160,5120]{3,2,1,0:T(8,128)(2,1)S(1)}, bf16[1,1,160,5120]{3,2,1,0:T(8,128)(2,1)}, u32[]{:S(2)}) copy-start(bf16[1,1,160,5120]{3,2,1,0:T(8,128)(2,1)} %param.11) | copy-start | bytes 4915204
  7.8 26.1 %collective-permute-start.13 = (bf16[3,8,5120]{2,1,0:T(8,128)(2,1)}, bf16[3,8,5120]{2,1,0:T(8,128)(2,1)S(1)}, u32[]{:S(2)}, u32[]{:S(2)}) collective-permute-start(bf16[3,8,5120]{2,1,0:T(8,128)(2,1)} %get-tuple-element.71), channel_id=1, source_target_pairs={{0,8},{1,9},{2,10},{3,11},{4,12},{5,13},{6,14},{7,15},{8,16},{9,17... | collective-permute-start | bytes 737288 | tf_op jit(solution)/shard_map/ppermute | solution.py:522
  10.3 21.8 %collective-permute-start.9 = (bf16[2,8,5120]{2,1,0:T(8,128)(2,1)}, bf16[2,8,5120]{2,1,0:T(8,128)(2,1)S(1)}, u32[]{:S(2)}, u32[]{:S(2)}) collective-permute-start(bf16[2,8,5120]{2,1,0:T(8,128)(2,1)} %get-tuple-element.65), channel_id=1, source_target_pairs={{0,8},{1,9},{2,10},{3,11},{4,12},{5,13},{6,14},{7,15},{8,16},{9,17... | collective-permute-start | bytes 491528 | tf_op jit(solution)/shard_map/ppermute | solution.py:550
  11.8 24.6 %collective-permute-start.14 = (bf16[3,8,5120]{2,1,0:T(8,128)(2,1)}, bf16[3,8,5120]{2,1,0:T(8,128)(2,1)S(1)}, u32[]{:S(2)}, u32[]{:S(2)}) collective-permute-start(bf16[3,8,5120]{2,1,0:T(8,128)(2,1)} %get-tuple-element.72), channel_id=1, source_target_pairs={{0,10},{1,11},{2,8},{3,9},{4,14},{5,15},{6,12},{7,13},{8,18},{9,19... | collective-permute-start | bytes 737288 | tf_op jit(solution)/shard_map/ppermute | solution.py:522
  14.3 22.1 %collective-permute-start.15 = (bf16[3,8,5120]{2,1,0:T(8,128)(2,1)}, bf16[3,8,5120]{2,1,0:T(8,128)(2,1)S(1)}, u32[]{:S(2)}, u32[]{:S(2)}) collective-permute-start(bf16[3,8,5120]{2,1,0:T(8,128)(2,1)} %get-tuple-element.73), channel_id=1, source_target_pairs={{0,12},{1,13},{2,14},{3,15},{4,8},{5,9},{6,10},{7,11},{8,20},{9,21... | collective-permute-start | bytes 737288 | tf_op jit(solution)/shard_map/ppermute | solution.py:522
  32.1 24.2 %copy-start.3 = (bf16[2,8,5120]{2,1,0:T(8,128)(2,1)}, bf16[2,8,5120]{2,1,0:T(8,128)(2,1)S(1)}, u32[]{:S(2)}) copy-start(bf16[2,8,5120]{2,1,0:T(8,128)(2,1)S(1)} %collective-permute-done.9.refs_0_) | copy-start | bytes 491524
  32.1 6.1 %collective-permute-start.10 = (bf16[2,8,5120]{2,1,0:T(8,128)(2,1)S(1)}, bf16[2,8,5120]{2,1,0:T(8,128)(2,1)S(1)}, u32[]{:S(2)}, u32[]{:S(2)}) collective-permute-start(bf16[2,8,5120]{2,1,0:T(8,128)(2,1)S(1)} %collective-permute-done.9.refs_0_), channel_id=1, source_target_pairs={{0,2},{1,3},{2,0},{3,1},{4,6},{5,7},{6,4},{7,5},{8,10},{9,11},{10,... | collective-permute-start | bytes 491528 | tf_op jit(solution)/shard_map/ppermute | solution.py:559
  33.9 12.5 %collective-permute-start.16 = (bf16[3,8,5120]{2,1,0:T(8,128)(2,1)}, bf16[3,8,5120]{2,1,0:T(8,128)(2,1)S(1)}, u32[]{:S(2)}, u32[]{:S(2)}) collective-permute-start(bf16[3,8,5120]{2,1,0:T(8,128)(2,1)} %get-tuple-element.74), channel_id=1, source_target_pairs={{0,14},{1,15},{2,12},{3,13},{4,10},{5,11},{6,8},{7,9},{8,22},{9,23... | collective-permute-start | bytes 737288 | tf_op jit(solution)/shard_map/ppermute | solution.py:522
  36.4 16.2 %collective-permute-start.17 = (bf16[3,8,5120]{2,1,0:T(8,128)(2,1)S(1)}, bf16[3,8,5120]{2,1,0:T(8,128)(2,1)S(1)}, u32[]{:S(2)}, u32[]{:S(2)}) collective-permute-start(bf16[3,8,5120]{2,1,0:T(8,128)(2,1)S(1)} %collective-permute-done.13.refs_2_), channel_id=1, source_target_pairs={{0,1},{1,0},{2,3},{3,2},{4,5},{5,4},{6,7},{7,6},{8,9},{9,8},{10,11... | collective-permute-start | bytes 737288 | tf_op jit(solution)/shard_map/ppermute | solution.py:45
  36.4 18.7 %collective-permute-start.18 = (bf16[3,8,5120]{2,1,0:T(8,128)(2,1)S(1)}, bf16[3,8,5120]{2,1,0:T(8,128)(2,1)S(1)}, u32[]{:S(2)}, u32[]{:S(2)}) collective-permute-start(bf16[3,8,5120]{2,1,0:T(8,128)(2,1)S(1)} %collective-permute-done.14.refs_3_), channel_id=1, source_target_pairs={{0,1},{1,0},{2,3},{3,2},{4,5},{5,4},{6,7},{7,6},{8,9},{9,8},{10,11... | collective-permute-start | bytes 737288 | tf_op jit(solution)/shard_map/ppermute | solution.py:45
  38.2 18.1 %copy-start.5 = (bf16[2,8,5120]{2,1,0:T(8,128)(2,1)}, bf16[2,8,5120]{2,1,0:T(8,128)(2,1)S(1)}, u32[]{:S(2)}) copy-start(bf16[2,8,5120]{2,1,0:T(8,128)(2,1)S(1)} %collective-permute-done.10.refs_1_) | copy-start | bytes 491524
  38.2 8.2 %collective-permute-start.11 = (bf16[2,8,5120]{2,1,0:T(8,128)(2,1)S(1)}, bf16[2,8,5120]{2,1,0:T(8,128)(2,1)S(1)}, u32[]{:S(2)}, u32[]{:S(2)}) collective-permute-start(bf16[2,8,5120]{2,1,0:T(8,128)(2,1)S(1)} %collective-permute-done.9.refs_0_), channel_id=1, source_target_pairs={{0,1},{1,0},{2,3},{3,2},{4,5},{5,4},{6,7},{7,6},{8,9},{9,8},{10,11... | collective-permute-start | bytes 491528 | tf_op jit(solution)/shard_map/ppermute | solution.py:45
  38.2 9.4 %collective-permute-start.12 = (bf16[2,8,5120]{2,1,0:T(8,128)(2,1)S(1)}, bf16[2,8,5120]{2,1,0:T(8,128)(2,1)S(1)}, u32[]{:S(2)}, u32[]{:S(2)}) collective-permute-start(bf16[2,8,5120]{2,1,0:T(8,128)(2,1)S(1)} %collective-permute-done.10.refs_1_), channel_id=1, source_target_pairs={{0,1},{1,0},{2,3},{3,2},{4,5},{5,4},{6,7},{7,6},{8,9},{9,8},{10,11... | collective-permute-start | bytes 491528 | tf_op jit(solution)/shard_map/ppermute | solution.py:45
  46.4 9.9 %collective-permute-start.19 = (bf16[3,8,5120]{2,1,0:T(8,128)(2,1)S(1)}, bf16[3,8,5120]{2,1,0:T(8,128)(2,1)S(1)}, u32[]{:S(2)}, u32[]{:S(2)}) collective-permute-start(bf16[3,8,5120]{2,1,0:T(8,128)(2,1)S(1)} %collective-permute-done.15.refs_4_), channel_id=1, source_target_pairs={{0,1},{1,0},{2,3},{3,2},{4,5},{5,4},{6,7},{7,6},{8,9},{9,8},{10,11... | collective-permute-start | bytes 737288 | tf_op jit(solution)/shard_map/ppermute | solution.py:45
  46.4 0.7 copy-start.7
  47.1 18.8 %collective-permute-start.22 = (bf16[3,8,5120]{2,1,0:T(8,128)(2,1)S(1)}, bf16[3,8,5120]{2,1,0:T(8,128)(2,1)}, u32[]{:S(2)}, u32[]{:S(2)}) collective-permute-start(bf16[3,8,5120]{2,1,0:T(8,128)(2,1)S(1)} %get-tuple-element.75), channel_id=1, source_target_pairs={{0,8},{1,9},{2,10},{3,11},{4,12},{5,13},{6,14},{7,15},{8,16},{9,17... | collective-permute-start | bytes 737288 | tf_op jit(solution)/shard_map/ppermute | solution.py:522
  47.6 0.7 copy-start.9
  48.3 17.7 %collective-permute-start.23 = (bf16[3,8,5120]{2,1,0:T(8,128)(2,1)S(1)}, bf16[3,8,5120]{2,1,0:T(8,128)(2,1)}, u32[]{:S(2)}, u32[]{:S(2)}) collective-permute-start(bf16[3,8,5120]{2,1,0:T(8,128)(2,1)S(1)} %get-tuple-element.76), channel_id=1, source_target_pairs={{0,10},{1,11},{2,8},{3,9},{4,14},{5,15},{6,12},{7,13},{8,18},{9,19... | collective-permute-start | bytes 737288 | tf_op jit(solution)/shard_map/ppermute | solution.py:522
  52.6 22.2 %collective-permute-start.24 = (bf16[3,8,5120]{2,1,0:T(8,128)(2,1)S(1)}, bf16[3,8,5120]{2,1,0:T(8,128)(2,1)}, u32[]{:S(2)}, u32[]{:S(2)}) collective-permute-start(bf16[3,8,5120]{2,1,0:T(8,128)(2,1)S(1)} %get-tuple-element.77), channel_id=1, source_target_pairs={{0,12},{1,13},{2,14},{3,15},{4,8},{5,9},{6,10},{7,11},{8,20},{9,21... | collective-permute-start | bytes 737288 | tf_op jit(solution)/shard_map/ppermute | solution.py:522
  55.1 0.7 copy-start.1
  55.8 28.3 %copy-start.2 = (bf16[3,8,5120]{2,1,0:T(8,128)(2,1)S(1)}, bf16[3,8,5120]{2,1,0:T(8,128)(2,1)}, u32[]{:S(2)}) copy-start(bf16[3,8,5120]{2,1,0:T(8,128)(2,1)} %copy-done.1) | copy-start | bytes 737284
  55.8 18.9 %collective-permute-start.25 = (bf16[3,8,5120]{2,1,0:T(8,128)(2,1)S(1)}, bf16[3,8,5120]{2,1,0:T(8,128)(2,1)}, u32[]{:S(2)}, u32[]{:S(2)}) collective-permute-start(bf16[3,8,5120]{2,1,0:T(8,128)(2,1)S(1)} %get-tuple-element.78), channel_id=1, source_target_pairs={{0,14},{1,15},{2,12},{3,13},{4,10},{5,11},{6,8},{7,9},{8,22},{9,23... | collective-permute-start | bytes 737288 | tf_op jit(solution)/shard_map/ppermute | solution.py:522
  56.4 27.7 %collective-permute-start.20 = (bf16[3,8,5120]{2,1,0:T(8,128)(2,1)S(1)}, bf16[3,8,5120]{2,1,0:T(8,128)(2,1)}, u32[]{:S(2)}, u32[]{:S(2)}) collective-permute-start(bf16[3,8,5120]{2,1,0:T(8,128)(2,1)S(1)} %collective-permute-done.16.refs_5_), channel_id=1, source_target_pairs={{0,1},{1,0},{2,3},{3,2},{4,5},{5,4},{6,7},{7,6},{8,9},{9,8},{10,11... | collective-permute-start | bytes 737288 | tf_op jit(solution)/shard_map/ppermute | solution.py:45
  65.9 18.1 %collective-permute-start.26 = (bf16[3,8,5120]{2,1,0:T(8,128)(2,1)}, bf16[3,8,5120]{2,1,0:T(8,128)(2,1)}, u32[]{:S(2)}, u32[]{:S(2)}) collective-permute-start(bf16[3,8,5120]{2,1,0:T(8,128)(2,1)} %collective-permute-done.22.refs_10_), channel_id=1, source_target_pairs={{0,1},{1,0},{2,3},{3,2},{4,5},{5,4},{6,7},{7,6},{8,9},{9,8},{10,11... | collective-permute-start | bytes 737288 | tf_op jit(solution)/shard_map/ppermute | solution.py:45
  65.9 18.1 %collective-permute-start.27 = (bf16[3,8,5120]{2,1,0:T(8,128)(2,1)}, bf16[3,8,5120]{2,1,0:T(8,128)(2,1)}, u32[]{:S(2)}, u32[]{:S(2)}) collective-permute-start(bf16[3,8,5120]{2,1,0:T(8,128)(2,1)} %collective-permute-done.23.refs_11_), channel_id=1, source_target_pairs={{0,1},{1,0},{2,3},{3,2},{4,5},{5,4},{6,7},{7,6},{8,9},{9,8},{10,11... | collective-permute-start | bytes 737288 | tf_op jit(solution)/shard_map/ppermute | solution.py:45
  74.8 9.3 %collective-permute-start.28 = (bf16[3,8,5120]{2,1,0:T(8,128)(2,1)}, bf16[3,8,5120]{2,1,0:T(8,128)(2,1)}, u32[]{:S(2)}, u32[]{:S(2)}) collective-permute-start(bf16[3,8,5120]{2,1,0:T(8,128)(2,1)} %collective-permute-done.24.refs_12_), channel_id=1, source_target_pairs={{0,1},{1,0},{2,3},{3,2},{4,5},{5,4},{6,7},{7,6},{8,9},{9,8},{10,11... | collective-permute-start | bytes 737288 | tf_op jit(solution)/shard_map/ppermute | solution.py:45
  74.8 9.3 %collective-permute-start.29 = (bf16[3,8,5120]{2,1,0:T(8,128)(2,1)}, bf16[3,8,5120]{2,1,0:T(8,128)(2,1)}, u32[]{:S(2)}, u32[]{:S(2)}) collective-permute-start(bf16[3,8,5120]{2,1,0:T(8,128)(2,1)} %collective-permute-done.25.refs_13_), channel_id=1, source_target_pairs={{0,1},{1,0},{2,3},{3,2},{4,5},{5,4},{6,7},{7,6},{8,9},{9,8},{10,11... | collective-permute-start | bytes 737288 | tf_op jit(solution)/shard_map/ppermute | solution.py:45
  77.5 0.9 copy-start.4
  78.4 0.9 copy-start.6
  79.3 0.9 copy-start.8
  80.3 0.9 copy-start.10
  81.2 2.9 %copy-start.11 = (s32[24]{0:T(128)S(1)}, s32[24]{0:T(128)}, u32[]{:S(2)}) copy-start(s32[24]{0:T(128)} %get-tuple-element.69.refs_0_) | copy-start | bytes 292
  81.2 3.0 %copy-start.12 = (s32[24]{0:T(128)S(1)}, s32[24]{0:T(128)}, u32[]{:S(2)}) copy-start(s32[24]{0:T(128)} %get-tuple-element.70.refs_1_) | copy-start | bytes 292
  93.9 1.7 %collective-permute-start.30 = (bf16[4,64,640]{2,1,0:T(8,128)(2,1)S(1)}, bf16[4,64,640]{2,1,0:T(8,128)(2,1)S(1)}, u32[]{:S(2)}, u32[]{:S(2)}) collective-permute-start(bf16[4,64,640]{2,1,0:T(8,128)(2,1)S(1)} %get-tuple-element.83), channel_id=1, source_target_pairs={{0,1},{1,0},{2,3},{3,2},{4,5},{5,4},{6,7},{7,6},{8,9},{9,8},{10,11... | collective-permute-start | bytes 983048 | tf_op jit(solution)/shard_map/ppermute | solution.py:45
  95.6 8.8 %collective-permute-start.31 = (bf16[64,640]{1,0:T(8,128)(2,1)S(1)}, bf16[64,640]{1,0:T(8,128)(2,1)S(1)}, u32[]{:S(2)}, u32[]{:S(2)}) collective-permute-start(bf16[64,640]{1,0:T(8,128)(2,1)S(1)} %get-tuple-element.84), channel_id=1, source_target_pairs={{0,30},{1,31},{2,28},{3,29},{4,26},{5,27},{6,24},{7,25},{8,6},{9,7... | collective-permute-start | bytes 245768 | tf_op jit(solution)/shard_map/ppermute | solution.py:589
  98.3 10.5 %collective-permute-start.32 = (bf16[64,640]{1,0:T(8,128)(2,1)S(1)}, bf16[64,640]{1,0:T(8,128)(2,1)S(1)}, u32[]{:S(2)}, u32[]{:S(2)}) collective-permute-start(bf16[64,640]{1,0:T(8,128)(2,1)S(1)} %get-tuple-element.85), channel_id=1, source_target_pairs={{0,28},{1,29},{2,30},{3,31},{4,24},{5,25},{6,26},{7,27},{8,4},{9,5... | collective-permute-start | bytes 245768 | tf_op jit(solution)/shard_map/ppermute | solution.py:589
  102.8 6.3 %collective-permute-start.33 = (bf16[64,640]{1,0:T(8,128)(2,1)S(1)}, bf16[64,640]{1,0:T(8,128)(2,1)S(1)}, u32[]{:S(2)}, u32[]{:S(2)}) collective-permute-start(bf16[64,640]{1,0:T(8,128)(2,1)S(1)} %get-tuple-element.86), channel_id=1, source_target_pairs={{0,26},{1,27},{2,24},{3,25},{4,30},{5,31},{6,28},{7,29},{8,2},{9,3... | collective-permute-start | bytes 245768 | tf_op jit(solution)/shard_map/ppermute | solution.py:589
  104.1 6.4 %collective-permute-start.34 = (bf16[64,640]{1,0:T(8,128)(2,1)S(1)}, bf16[64,640]{1,0:T(8,128)(2,1)S(1)}, u32[]{:S(2)}, u32[]{:S(2)}) collective-permute-start(bf16[64,640]{1,0:T(8,128)(2,1)S(1)} %get-tuple-element.87), channel_id=1, source_target_pairs={{0,24},{1,25},{2,26},{3,27},{4,28},{5,29},{6,30},{7,31},{8,0},{9,1... | collective-permute-start | bytes 245768 | tf_op jit(solution)/shard_map/ppermute | solution.py:589
